TPU v7x, 32 devices: a whole 2x2x4 slice. The times are simulated.
32 devices in a mesh: dp: 2 (over y), seq: 16 (over z, x, core).
Axes of the slice: x: 2, y: 2, z: 4, core: 2. Of those that a mesh axis runs over, the one named last changes fastest.
Arguments:
- tokens: bfloat16 [4, 2048, 768], P('dp', 'seq'), may hold values from -6 to 6
- segments: int32 [4, 2048], P('dp', 'seq'), may hold values from 0 to 1, never falling along the last dimension, each value on 1 to 2000 neighbouring positions
- qkv_weight: bfloat16 [768, 2304], P(('dp', 'seq')), may hold values from -0.21875 to 0.21875
- out_weight: bfloat16 [768, 768], P(('dp', 'seq')), may hold values from -4 to 4
- up_weight: bfloat16 [768, 3072], P(('dp', 'seq')), may hold values from -0.21875 to 0.21875
- down_weight: bfloat16 [3072, 768], P(('dp', 'seq')), may hold values from -0.109375 to 0.109375
- query_bias: bfloat16 [768], P(('dp', 'seq')), may hold values from -3 to 3
- value_bias: bfloat16 [768], P(('dp', 'seq')), may hold values from -3 to 3
- out_bias: bfloat16 [768], P(('dp', 'seq')), may hold values from -3 to 3
- first_gain: bfloat16 [768], P(('dp', 'seq')), may hold values from 0.099609375 to 1.8984375
- first_shift: bfloat16 [768], P(('dp', 'seq')), may hold values from -3 to 3
- up_bias: bfloat16 [3072], P(('dp', 'seq')), may hold values from -3 to 3
- down_bias: bfloat16 [768], P(('dp', 'seq')), may hold values from -3 to 3
- second_gain: bfloat16 [768], P(('dp', 'seq')), may hold values from 0.099609375 to 1.8984375
- second_shift: bfloat16 [768], P(('dp', 'seq')), may hold values from -3 to 3
- cotangent: bfloat16 [4, 2048, 768], P('dp', 'seq'), may hold values from -6 to 6
Outputs:
- layer_output: bfloat16 [4, 2048, 768], P('dp', 'seq')
- input_grad: bfloat16 [4, 2048, 768], P('dp', 'seq')
- grad_qkv_weight: float32 [768, 2304], P(('dp', 'seq'))
- grad_out_weight: float32 [768, 768], P(('dp', 'seq'))
- grad_up_weight: float32 [768, 3072], P(('dp', 'seq'))
- grad_down_weight: float32 [3072, 768], P(('dp', 'seq'))
- grad_query_bias: float32 [768], P(('dp', 'seq'))
- grad_value_bias: float32 [768], P(('dp', 'seq'))
- grad_out_bias: float32 [768], P(('dp', 'seq'))
- grad_first_gain: float32 [768], P(('dp', 'seq'))
- grad_first_shift: float32 [768], P(('dp', 'seq'))
- grad_up_bias: float32 [3072], P(('dp', 'seq'))
- grad_down_bias: float32 [768], P(('dp', 'seq'))
- grad_second_gain: float32 [768], P(('dp', 'seq'))
- grad_second_shift: float32 [768], P(('dp', 'seq'))
Inputs may be any that keep to these rules, and one draw needn't show every extreme that they name: `segments`: in each sequence segment numbers never fall from one token to the next, every number up to 1 appears, each document holds at most 2000 tokens.
All inputs are finite; a program needn't handle non-finite values.
Results may differ from a plain program's by a relative error of at most 0.017.
Values may be sent and summed in bfloat16 or wider, within the bound.
No kernel may reach another device: no remote copies, remote signals or barrier semaphores. Data moves between devices by JAX's collectives and lax.ppermute only.
A program may use at most 320 MiB of HBM per device.

v0:
```python
import jax
import jax.numpy as jnp
from jax import lax
from jax.sharding import PartitionSpec as P

HEADS = 12
HEAD_DIM = 64
FF = 3072
DOC_MOST = 2000


EPS = 1e-12
NEGATIVE = -1e30


def norm_layer(summed, gain_row, shift_row):
    average = jnp.mean(summed, axis=-1, keepdims=True)
    centred = summed - average
    variance = jnp.mean(centred * centred, axis=-1, keepdims=True)
    return centred * lax.rsqrt(variance + EPS) * gain_row + shift_row


def exact_gelu(inner_rows):
    return jax.nn.gelu(inner_rows, approximate=False)


def same_value(state_pair):
    return state_pair


def head_split(matrix):
    return matrix.reshape(matrix.shape[0], HEADS, HEAD_DIM)


def block_scores(query_heads, key_rows):
    return (
        jnp.einsum(
            "qhd,khd->hqk", query_heads, head_split(key_rows), preferred_element_type=jnp.float32
        )
        * 0.125
    )


def probabilities(query_heads, key_stack, block_index, allowed, log_total):
    scores = block_scores(query_heads, key_stack[block_index, :, : HEADS * HEAD_DIM])
    return jnp.where(allowed[None], jnp.exp(scores - log_total[:, :, None]), 0.0)


def block_mask(query_segment, key_segments, block_index):
    return query_segment[:, None] == key_segments[block_index][None, :]


def log_totals(query_heads, key_stack, key_segments, query_segment):
    row_count = query_heads.shape[0]

    def log_visit(block_index, carry_state):
        allowed = block_mask(query_segment, key_segments, block_index)

        def log_compute(state_pair):
            top_now, total_now = state_pair
            scores = jnp.where(
                allowed[None],
                block_scores(query_heads, key_stack[block_index, :, : HEADS * HEAD_DIM]),
                NEGATIVE,
            )
            top_new = jnp.maximum(top_now, jnp.max(scores, axis=-1))
            expon_rows = jnp.where(allowed[None], jnp.exp(scores - top_new[:, :, None]), 0.0)
            return (top_new, total_now * jnp.exp(top_now - top_new) + jnp.sum(expon_rows, axis=-1))

        return lax.cond(jnp.any(allowed), log_compute, same_value, carry_state)

    initial = (
        jnp.full((HEADS, row_count), NEGATIVE, jnp.float32),
        jnp.zeros((HEADS, row_count), jnp.float32),
    )
    top_final, total_final = lax.fori_loop(0, key_stack.shape[0], log_visit, initial)
    return top_final + jnp.log(total_final)


def attend_values(query_heads, key_stack, key_segments, query_segment, log_total):
    model_width = HEADS * HEAD_DIM

    def attend_visit(block_index, running):
        allowed = block_mask(query_segment, key_segments, block_index)

        def attend_compute(running_in):
            main_sum, rest_sum = running_in
            weights_block = probabilities(query_heads, key_stack, block_index, allowed, log_total)
            weights_low = weights_block.astype(jnp.bfloat16)
            weights_rest = (weights_block - weights_low.astype(jnp.float32)).astype(jnp.bfloat16)
            value_heads = head_split(key_stack[block_index, :, model_width:])
            main_new = main_sum + jnp.einsum(
                "hqk,khd->qhd", weights_low, value_heads, preferred_element_type=jnp.float32
            )
            rest_new = rest_sum + jnp.einsum(
                "hqk,khd->qhd", weights_rest, value_heads, preferred_element_type=jnp.float32
            )
            return (main_new, rest_new)

        return lax.cond(jnp.any(allowed), attend_compute, same_value, running)

    zero_heads = jnp.zeros(query_heads.shape, jnp.float32)
    main_sum, rest_sum = lax.fori_loop(
        0, key_stack.shape[0], attend_visit, (zero_heads, zero_heads)
    )
    return (main_sum.reshape(query_heads.shape[0], model_width), main_sum + rest_sum)


def attention_back(
    query_heads, grad_heads, key_stack, key_segments, query_segment, log_total, exact_heads
):
    model_width = HEADS * HEAD_DIM
    row_count = query_heads.shape[0]
    delta_rows = jnp.einsum("qhd,qhd->hq", grad_heads.astype(jnp.float32), exact_heads)

    def grad_visit(block_index, carry_state):
        allowed = block_mask(query_segment, key_segments, block_index)

        def grad_compute(state_pair):
            grad_query_in, contrib_in = state_pair
            weights_block = probabilities(query_heads, key_stack, block_index, allowed, log_total)
            key_heads = head_split(key_stack[block_index, :, :model_width])
            value_heads = head_split(key_stack[block_index, :, model_width:])
            grad_probs = jnp.einsum(
                "qhd,khd->hqk", grad_heads, value_heads, preferred_element_type=jnp.float32
            )
            grad_scores = (weights_block * (grad_probs - delta_rows[:, :, None])).astype(
                jnp.bfloat16
            )
            grad_query_new = grad_query_in + jnp.einsum(
                "hqk,khd->qhd", grad_scores, key_heads, preferred_element_type=jnp.float32
            )
            grad_keys = (
                jnp.einsum(
                    "hqk,qhd->khd", grad_scores, query_heads, preferred_element_type=jnp.float32
                )
                * 0.125
            )
            grad_values = jnp.einsum(
                "hqk,qhd->khd",
                weights_block.astype(jnp.bfloat16),
                grad_heads,
                preferred_element_type=jnp.float32,
            )
            joined = jnp.concatenate(
                [
                    grad_keys.reshape(row_count, model_width),
                    grad_values.reshape(row_count, model_width),
                ],
                axis=1,
            )
            return (
                grad_query_new,
                lax.dynamic_update_index_in_dim(contrib_in, joined, block_index, 0),
            )

        return lax.cond(jnp.any(allowed), grad_compute, same_value, carry_state)

    initial = (
        jnp.zeros(query_heads.shape, jnp.float32),
        jnp.zeros((key_stack.shape[0], row_count, 2 * model_width), jnp.float32),
    )
    grad_query, contrib = lax.fori_loop(0, key_stack.shape[0], grad_visit, initial)
    return ((grad_query * 0.125).reshape(row_count, model_width), contrib)


def weight_grad(left_rows, right_rows):
    return jnp.einsum("rk,rn->kn", left_rows, right_rows, preferred_element_type=jnp.float32)


def data_grad(grad_rows, weight_full):
    return jnp.einsum("rn,kn->rk", grad_rows, weight_full, preferred_element_type=jnp.float32)


def column_sum(rows_low):
    return jnp.sum(rows_low.astype(jnp.float32), axis=0)


def local(
    tokens,
    segments,
    qkv_weight,
    out_weight,
    up_weight,
    down_weight,
    query_bias,
    value_bias,
    out_bias,
    first_gain,
    first_shift,
    up_bias,
    down_bias,
    second_gain,
    second_shift,
    cotangent,
):
    batch_count, row_count, model_width = tokens.shape
    seq_count = lax.axis_size("seq")
    reach = min((DOC_MOST + row_count - 2) // row_count, seq_count - 1)
    window = 2 * reach + 1
    position = lax.axis_index("seq")
    every_segment = lax.all_gather(segments, "seq", axis=1, tiled=True)
    padded_segment = jnp.pad(
        every_segment, ((0, 0), (reach * row_count, reach * row_count)), constant_values=-1
    )
    totals = [
        jnp.zeros((model_width, 3 * model_width), jnp.float32),
        jnp.zeros((model_width, model_width), jnp.float32),
        jnp.zeros((model_width, FF), jnp.float32),
        jnp.zeros((FF, model_width), jnp.float32),
        jnp.zeros((model_width,), jnp.float32),
        jnp.zeros((model_width,), jnp.float32),
        jnp.zeros((model_width,), jnp.float32),
        jnp.zeros((model_width,), jnp.float32),
        jnp.zeros((model_width,), jnp.float32),
        jnp.zeros((FF,), jnp.float32),
        jnp.zeros((model_width,), jnp.float32),
        jnp.zeros((model_width,), jnp.float32),
        jnp.zeros((model_width,), jnp.float32),
    ]
    outputs = []
    input_grads = []
    for micro in range(batch_count):
        weights_now = (
            lax.all_gather(qkv_weight, ("dp", "seq"), axis=0, tiled=True),
            lax.all_gather(out_weight, ("dp", "seq"), axis=0, tiled=True),
            lax.all_gather(up_weight, ("dp", "seq"), axis=0, tiled=True),
            lax.all_gather(down_weight, ("dp", "seq"), axis=0, tiled=True),
            lax.all_gather(query_bias, ("dp", "seq"), axis=0, tiled=True),
            lax.all_gather(value_bias, ("dp", "seq"), axis=0, tiled=True),
            lax.all_gather(out_bias, ("dp", "seq"), axis=0, tiled=True),
            lax.all_gather(first_gain, ("dp", "seq"), axis=0, tiled=True),
            lax.all_gather(first_shift, ("dp", "seq"), axis=0, tiled=True),
            lax.all_gather(up_bias, ("dp", "seq"), axis=0, tiled=True),
            lax.all_gather(down_bias, ("dp", "seq"), axis=0, tiled=True),
            lax.all_gather(second_gain, ("dp", "seq"), axis=0, tiled=True),
            lax.all_gather(second_shift, ("dp", "seq"), axis=0, tiled=True),
        )
        (
            qkv_full,
            out_full,
            up_full,
            down_full,
            query_b,
            value_b,
            out_b,
            first_g,
            first_s,
            up_b,
            down_b,
            second_g,
            second_s,
        ) = weights_now
        inputs = tokens[micro]
        merged = jnp.dot(inputs, qkv_full, preferred_element_type=jnp.float32)
        query = (merged[:, :model_width] + query_b.astype(jnp.float32)).astype(jnp.bfloat16)
        keys_now = merged[:, model_width : 2 * model_width].astype(jnp.bfloat16)
        values_now = (merged[:, 2 * model_width :] + value_b.astype(jnp.float32)).astype(
            jnp.bfloat16
        )
        whole_keys = lax.all_gather(
            jnp.concatenate([keys_now, values_now], axis=1), "seq", axis=0, tiled=True
        )
        padded = jnp.pad(whole_keys, ((reach * row_count, reach * row_count), (0, 0)))
        picked = lax.dynamic_slice_in_dim(padded, position * row_count, window * row_count, 0)
        key_stack = picked.reshape(window, row_count, 2 * model_width)
        key_segments = lax.dynamic_slice_in_dim(
            padded_segment[micro], position * row_count, window * row_count, 0
        ).reshape(window, row_count)
        query_segment = segments[micro]
        query_heads = head_split(query)
        log_total = log_totals(query_heads, key_stack, key_segments, query_segment)
        attended_f, exact_heads = attend_values(
            query_heads, key_stack, key_segments, query_segment, log_total
        )
        attended = attended_f.astype(jnp.bfloat16)
        branch = jnp.dot(attended, out_full, preferred_element_type=jnp.float32) + out_b.astype(
            jnp.float32
        )
        hidden, first_pull = jax.vjp(
            norm_layer,
            inputs.astype(jnp.float32) + branch,
            first_g.astype(jnp.float32),
            first_s.astype(jnp.float32),
        )
        hidden_low = hidden.astype(jnp.bfloat16)
        inner_rows = jnp.dot(hidden_low, up_full, preferred_element_type=jnp.float32) + up_b.astype(
            jnp.float32
        )
        activated, gelu_pull = jax.vjp(exact_gelu, inner_rows)
        activated_low = activated.astype(jnp.bfloat16)
        second = jnp.dot(
            activated_low, down_full, preferred_element_type=jnp.float32
        ) + down_b.astype(jnp.float32)
        output, second_pull = jax.vjp(
            norm_layer, hidden + second, second_g.astype(jnp.float32), second_s.astype(jnp.float32)
        )
        outputs.append(output.astype(jnp.bfloat16))
        back_weights = (
            lax.all_gather(qkv_weight, ("dp", "seq"), axis=0, tiled=True),
            lax.all_gather(out_weight, ("dp", "seq"), axis=0, tiled=True),
            lax.all_gather(up_weight, ("dp", "seq"), axis=0, tiled=True),
            lax.all_gather(down_weight, ("dp", "seq"), axis=0, tiled=True),
            lax.all_gather(query_bias, ("dp", "seq"), axis=0, tiled=True),
            lax.all_gather(value_bias, ("dp", "seq"), axis=0, tiled=True),
            lax.all_gather(out_bias, ("dp", "seq"), axis=0, tiled=True),
            lax.all_gather(first_gain, ("dp", "seq"), axis=0, tiled=True),
            lax.all_gather(first_shift, ("dp", "seq"), axis=0, tiled=True),
            lax.all_gather(up_bias, ("dp", "seq"), axis=0, tiled=True),
            lax.all_gather(down_bias, ("dp", "seq"), axis=0, tiled=True),
            lax.all_gather(second_gain, ("dp", "seq"), axis=0, tiled=True),
            lax.all_gather(second_shift, ("dp", "seq"), axis=0, tiled=True),
        )
        qkv_full, out_full, up_full, down_full = (
            back_weights[0],
            back_weights[1],
            back_weights[2],
            back_weights[3],
        )
        grad_sum2, grad_gain2, grad_shift2 = second_pull(cotangent[micro].astype(jnp.float32))
        grad_second = grad_sum2.astype(jnp.bfloat16)
        (grad_inner_f,) = gelu_pull(data_grad(grad_second, down_full))
        grad_inner = grad_inner_f.astype(jnp.bfloat16)
        grad_hidden = grad_sum2 + data_grad(grad_inner, up_full)
        grad_sum1, grad_gain1, grad_shift1 = first_pull(grad_hidden)
        grad_branch = grad_sum1.astype(jnp.bfloat16)
        grad_attended = data_grad(grad_branch, out_full).astype(jnp.bfloat16)
        grad_query_f, contrib = attention_back(
            query_heads,
            head_split(grad_attended),
            key_stack,
            key_segments,
            query_segment,
            log_total,
            exact_heads,
        )
        block_ids = position - reach + jnp.arange(window, dtype=jnp.int32)
        inside = (block_ids >= 0) & (block_ids < seq_count)
        canvas = jnp.zeros((seq_count, row_count, 2 * model_width), jnp.float32)
        canvas = canvas.at[jnp.clip(block_ids, 0, seq_count - 1)].add(
            jnp.where(inside[:, None, None], contrib, 0.0)
        )
        canvas = canvas.reshape(seq_count * row_count, 2 * model_width)
        key_value_grad = lax.psum_scatter(canvas, "seq", scatter_dimension=0, tiled=True)
        grad_query = grad_query_f.astype(jnp.bfloat16)
        grad_value = key_value_grad[:, model_width:].astype(jnp.bfloat16)
        grad_merged = jnp.concatenate(
            [grad_query, key_value_grad[:, :model_width].astype(jnp.bfloat16), grad_value], axis=1
        )
        input_grads.append((grad_sum1 + data_grad(grad_merged, qkv_full)).astype(jnp.bfloat16))
        terms = [
            weight_grad(inputs, grad_merged),
            weight_grad(attended, grad_branch),
            weight_grad(hidden_low, grad_inner),
            weight_grad(activated_low, grad_second),
            column_sum(grad_query),
            column_sum(grad_value),
            column_sum(grad_branch),
            grad_gain1,
            grad_shift1,
            column_sum(grad_inner),
            column_sum(grad_second),
            grad_gain2,
            grad_shift2,
        ]
        totals = [total_item + term_item for total_item, term_item in zip(totals, terms)]
    scattered = (
        lax.psum_scatter(totals[0], ("dp", "seq"), scatter_dimension=0, tiled=True),
        lax.psum_scatter(totals[1], ("dp", "seq"), scatter_dimension=0, tiled=True),
        lax.psum_scatter(totals[2], ("dp", "seq"), scatter_dimension=0, tiled=True),
        lax.psum_scatter(totals[3], ("dp", "seq"), scatter_dimension=0, tiled=True),
        lax.psum_scatter(totals[4], ("dp", "seq"), scatter_dimension=0, tiled=True),
        lax.psum_scatter(totals[5], ("dp", "seq"), scatter_dimension=0, tiled=True),
        lax.psum_scatter(totals[6], ("dp", "seq"), scatter_dimension=0, tiled=True),
        lax.psum_scatter(totals[7], ("dp", "seq"), scatter_dimension=0, tiled=True),
        lax.psum_scatter(totals[8], ("dp", "seq"), scatter_dimension=0, tiled=True),
        lax.psum_scatter(totals[9], ("dp", "seq"), scatter_dimension=0, tiled=True),
        lax.psum_scatter(totals[10], ("dp", "seq"), scatter_dimension=0, tiled=True),
        lax.psum_scatter(totals[11], ("dp", "seq"), scatter_dimension=0, tiled=True),
        lax.psum_scatter(totals[12], ("dp", "seq"), scatter_dimension=0, tiled=True),
    )
    return (
        jnp.stack(outputs),
        jnp.stack(input_grads),
        scattered[0],
        scattered[1],
        scattered[2],
        scattered[3],
        scattered[4],
        scattered[5],
        scattered[6],
        scattered[7],
        scattered[8],
        scattered[9],
        scattered[10],
        scattered[11],
        scattered[12],
    )


def solution(mesh):
    in_specs = (
        P("dp", "seq", None),
        P("dp", "seq"),
        P(("dp", "seq"), None),
        P(("dp", "seq"), None),
        P(("dp", "seq"), None),
        P(("dp", "seq"), None),
        P(("dp", "seq")),
        P(("dp", "seq")),
        P(("dp", "seq")),
        P(("dp", "seq")),
        P(("dp", "seq")),
        P(("dp", "seq")),
        P(("dp", "seq")),
        P(("dp", "seq")),
        P(("dp", "seq")),
        P("dp", "seq", None),
    )
    out_specs = (
        P("dp", "seq", None),
        P("dp", "seq", None),
        P(("dp", "seq"), None),
        P(("dp", "seq"), None),
        P(("dp", "seq"), None),
        P(("dp", "seq"), None),
        P(("dp", "seq")),
        P(("dp", "seq")),
        P(("dp", "seq")),
        P(("dp", "seq")),
        P(("dp", "seq")),
        P(("dp", "seq")),
        P(("dp", "seq")),
        P(("dp", "seq")),
        P(("dp", "seq")),
    )
    return jax.shard_map(local, mesh=mesh, in_specs=in_specs, out_specs=out_specs, check_vma=False)
```

profile of v0, /device:TPU:0, one launch (start us, length us, event | category | flops | bytes accessed | tf_op | source)
XLA Modules:
  0.0 1755.6 jit_solution(1924055928529830880)
XLA Ops:
  15.5 42.9 %all-reduce.22 = (bf16[3072]{0:T(1024)(128)(2,1)S(1)}, bf16[768]{0:T(1024)(128)(2,1)S(1)}, bf16[768]{0:T(1024)(128)(2,1)S(1)}, bf16[768]{0:T(1024)(128)(2,1)S(1)...) all-reduce(bf16[3072]{0:T(1024)(128)(2,1)S(1)} %dynamic-update-slic, ...), channel_id=1, replica_groups=mesh['dp'=2,'seq'=16] {'dp','seq'}, use_global_device_ids=true, to_apply=%add.8 | all-reduce | flops 9216 | bytes 36864
  58.4 15.1 all-gather.7.cloned.1.call-done
  80.9 20.3 %all_gather.32 = s32[2,2048]{1,0:T(2,128)S(1)} all-gather(s32[2,128]{1,0:T(2,128)S(1)} %copy-done.57), channel_id=1, replica_groups=mesh['dp'=2,'seq'=16] {'seq'}, dimensions={1}, use_global_device_ids=true | all-gather | bytes 17408 | tf_op jit(solution)/shard_map/all_gather | solution.py:202
  102.8 35.8 %all-gather.9.cloned.1.call-done = bf16[2048,1536]{1,0:T(8,128)(2,1)} async-done(((bf16[128,1536]{1,0:T(8,128)(2,1)}), bf16[2048,1536]{1,0:T(8,128)(2,1)}) %all-gather.9.cloned.1.call-update) | async-done | bytes 6291472 | tf_op jit(solution)/shard_map/all_gather | solution.py:261
  138.7 63.0 %all-gather.17.cloned.1.call-done = bf16[2048,1536]{1,0:T(8,128)(2,1)} async-done(((bf16[128,1536]{1,0:T(8,128)(2,1)}), bf16[2048,1536]{1,0:T(8,128)(2,1)}) %all-gather.17.cloned.1.call-update) | async-done | bytes 6291472 | tf_op jit(solution)/shard_map/all_gather | solution.py:261
  201.7 19.1 %pad_dynamic-slice_fusion = (bf16[3968,1536]{1,0:T(8,128)(2,1)}, bf16[3968,1536]{1,0:T(8,128)(2,1)}) fusion(s32[]{:T(128)S(6)} %select_n.106, bf16[2048,1536]{1,0:T(8,128)(2,1)} %all-gather.17.cloned.1.call-done, bf16[2048,1536]{1,0:T(8,128)(2,1)} %all-gather.9.cloned.1.call-done), kind=kLoop, calls=%fused_computation.96 | loop fusion | bytes 36962308 | tf_op jit(solution)/shard_map/dynamic_slice | solution.py:265
  220.8 16.4 copy.92
  237.2 50.1 %while.92 = (s32[]{:T(128)}, f32[12,128]{1,0:T(8,128)S(1)}, f32[12,128]{1,0:T(8,128)S(1)}, s32[1,128]{1,0:T(1,128)S(1)}, s32[31,128]{1,0:T(8,128)S(1)}, /*index=...) while((s32[]{:T(128)}, f32[12,128]{1,0:T(8,128)S(1)}, ...), condition=%wide.region_22.23_spmd, body=%wide.region_16.22_spmd.sunk | while | flops 26381316 | bytes 2490589 | solution.py:76
  287.4 52.0 %while.93 = (s32[]{:T(128)}, f32[128,12,64]{0,2,1:T(8,128)S(1)}, f32[128,12,64]{0,2,1:T(8,128)S(1)}, s32[1,128]{1,0:T(1,128)S(1)}, s32[31,128]{1,0:T(8,128)S(1)}...) while((s32[]{:T(128)}, f32[128,12,64]{0,2,1:T(8,128)S(1)}, ...), condition=%wide.region_27.28_spmd, body=%wide.region_23.0_spmd.sunk | while | flops 77299712 | bytes 5546221 | solution.py:103
  341.6 8.4 multiply_convert_fusion
  350.0 37.1 %all-gather.15.cloned.1.call-done = bf16[3072,768]{1,0:T(8,128)(2,1)} async-done(((bf16[96,768]{1,0:T(8,128)(2,1)}), bf16[3072,768]{1,0:T(8,128)(2,1)}) %all-gather.15.cloned.1.call-update) | async-done | bytes 4718608 | tf_op jit(solution)/shard_map/all_gather | solution.py:228
  391.2 16.4 copy.89
  407.6 66.4 %while.90 = (s32[]{:T(128)}, f32[12,128]{1,0:T(8,128)S(1)}, f32[12,128]{1,0:T(8,128)S(1)}, s32[1,128]{1,0:T(1,128)S(1)}, s32[31,128]{1,0:T(8,128)S(1)}, /*index=...) while((s32[]{:T(128)}, f32[12,128]{1,0:T(8,128)S(1)}, f32[12,128]{1,0:T(8,128)S(1)}, ...), condition=%wide.region_6.7_spmd, body=%wide.region_0.6_spmd.sunk | while | flops 26381316 | bytes 2490589 | solution.py:76
  474.2 73.2 %while.91 = (s32[]{:T(128)}, f32[128,12,64]{0,2,1:T(8,128)S(1)}, f32[128,12,64]{0,2,1:T(8,128)S(1)}, s32[1,128]{1,0:T(1,128)S(1)}, s32[31,128]{1,0:T(8,128)S(1)}...) while((s32[]{:T(128)}, f32[128,12,64]{0,2,1:T(8,128)S(1)}, ...), condition=%wide.region_11.12_spmd, body=%wide.region_7.11_spmd.sunk | while | flops 77299712 | bytes 5546221 | solution.py:103
  573.2 10.9 broadcast.413.clone.1
  584.2 81.1 %while.95 = (s32[]{:T(128)}, f32[128,12,64]{0,2,1:T(8,128)S(1)}, f32[31,128,1536]{1,2,0:T(8,128)}, s32[1,128]{1,0:T(1,128)S(1)}, s32[31,128]{1,0:T(8,128)}, /*in...) while((s32[]{:T(128)}, f32[128,12,64]{0,2,1:T(8,128)S(1)}, ...), condition=%wide.region_51.52_spmd, body=%wide.region_47.51_spmd.sunk | while | flops 127631360 | bytes 8894737 | solution.py:163
  668.0 10.9 broadcast.413.clone
  678.9 120.8 %while.94 = (s32[]{:T(128)}, f32[128,12,64]{0,2,1:T(8,128)S(1)}, f32[31,128,1536]{1,2,0:T(8,128)}, s32[1,128]{1,0:T(1,128)S(1)}, s32[31,128]{1,0:T(8,128)}, /*in...) while((s32[]{:T(128)}, f32[128,12,64]{0,2,1:T(8,128)S(1)}, ...), condition=%wide.region_40.41_spmd, body=%wide.region_36.40_spmd.sunk | while | flops 127631360 | bytes 8894737 | solution.py:163
  799.8 32.1 %broadcast_select_fusion.1 = (f32[31,128,1536]{1,2,0:T(8,128)}, f32[31,128,1536]{1,2,0:T(8,128)}) fusion(f32[31,128,1536]{1,2,0:T(8,128)} %get-tuple-element.1085, pred[31]{0:T(512)(128)(4,1)S(1)} %copy-done.63, f32[31,128,1536]{1,2,0:T(8,128)} %get-tuple-element.1088), kind=kLoop, calls=%fused_computation.99 | loop fusion | flops 12189696 | bytes 97517600 | tf_op jit(solution)/shard_map/jit(_where)/select_n | solution.py:341
  831.9 24.5 %copy.95 = f32[31,128,1536]{2,1,0:T(8,128)} copy(f32[31,128,1536]{1,2,0:T(8,128)} %get-tuple-element.1488) | data formatting | bytes 48758784 | tf_op jit(solution)/shard_map/jit(_where)/select_n | solution.py:341
  856.4 6.2 broadcast.415.clone.1
  862.6 54.4 %scatter_fusion = f32[16,128,1536]{2,1,0:T(8,128)} fusion(f32[16,128,1536]{2,1,0:T(8,128)} %broadcast.415.clone.1, s32[31]{0:T(128)S(1)} %copy-done.61, f32[31,128,1536]{2,1,0:T(8,128)} %copy.95), kind=kCustom, calls=%fused_computation | custom fusion | flops 6094848 | bytes 73138304 | tf_op jit(solution)/shard_map/scatter-add | solution.py:340
  917.1 24.5 %copy.99 = f32[31,128,1536]{2,1,0:T(8,128)} copy(f32[31,128,1536]{1,2,0:T(8,128)} %get-tuple-element.1489) | data formatting | bytes 48758784 | tf_op jit(solution)/shard_map/jit(_where)/select_n | solution.py:341
  947.8 56.5 %scatter_fusion.1 = f32[16,128,1536]{2,1,0:T(8,128)} fusion(f32[16,128,1536]{2,1,0:T(8,128)} %broadcast.415.clone, s32[31]{0:T(128)S(1)} %copy-done.61, f32[31,128,1536]{2,1,0:T(8,128)} %copy.99), kind=kCustom, calls=%fused_computation.1 | custom fusion | flops 6094848 | bytes 73138304 | tf_op jit(solution)/shard_map/scatter-add | solution.py:340
  1024.5 72.8 %reduce-scatter.9.cloned.1.call-done = f32[128,1536]{1,0:T(8,128)} async-done(((f32[2048,1536]{1,0:T(8,128)}), f32[128,1536]{1,0:T(8,128)}) %reduce-scatter.9.cloned.1.call-update) | async-done | bytes 786448 | tf_op jit(solution)/shard_map/reduce_scatter | solution.py:344
  1098.4 137.1 %reduce-scatter.11.cloned.1.call-done = f32[128,1536]{1,0:T(8,128)} async-done(((f32[2048,1536]{1,0:T(8,128)}), f32[128,1536]{1,0:T(8,128)}) %reduce-scatter.11.cloned.1.call-update) | async-done | bytes 786448 | tf_op jit(solution)/shard_map/reduce_scatter | solution.py:344
  1241.9 8.1 copy.128
  1264.7 42.0 %all-reduce.21 = (f32[768]{0:T(1024)}, f32[768]{0:T(1024)}, f32[768]{0:T(1024)}, f32[768]{0:T(1024)}, f32[768]{0:T(1024)}, /*index=5*/f32[3072]{0:T(1024)}, f32[768]{0:T(1024)}, f32[768]{0:T(1024)}, f32[768]{0:T(1024)}) all-reduce(f32[768]{0:T(1024)S(1)} %add.526, ...), channel_id=8, replica_groups=mesh['dp'=2,'seq'=16] {'dp','seq'}, use_global_device_ids=true, to_apply=%region_60.61.clone | all-reduce | flops 9216 | bytes 73728
  1322.9 17.4 reduce-scatter.13.cloned.1.call-done
  1340.3 141.9 %reduce-scatter.15.cloned.1.call-done = f32[24,3072]{1,0:T(8,128)} async-done(((f32[768,3072]{1,0:T(8,128)}), f32[24,3072]{1,0:T(8,128)}) %reduce-scatter.15.cloned.1.call-update) | async-done | bytes 294928 | tf_op jit(solution)/shard_map/reduce_scatter | solution.py:370
  1482.2 141.6 %reduce-scatter.17.cloned.1.call-done = f32[96,768]{1,0:T(8,128)} async-done(((f32[3072,768]{1,0:T(8,128)}), f32[96,768]{1,0:T(8,128)}) %reduce-scatter.17.cloned.1.call-update) | async-done | bytes 294928 | tf_op jit(solution)/shard_map/reduce_scatter | solution.py:371
  1623.8 124.6 %reduce-scatter.19.cloned.1.call-done = f32[24,2304]{1,0:T(8,128)} async-done(((f32[768,2304]{1,0:T(8,128)}), f32[24,2304]{1,0:T(8,128)}) %reduce-scatter.19.cloned.1.call-update) | async-done | bytes 221200
  (1188 shorter events, 567.1 us)
Async XLA Ops:
  7.2 66.4 %all-gather.7.cloned.1.call-start = ((), (), s32[]{:S(2)}) async-start(), calls=%async_computation.6 | async-start | bytes 3649536 | tf_op jit(solution)/shard_map/all_gather | solution.py:225
  7.9 130.7 %all-gather.9.cloned.1.call-start = ((), (), s32[]{:S(2)}) async-start(), calls=%async_computation.7 | async-start | bytes 6684672 | tf_op jit(solution)/shard_map/all_gather | solution.py:261
  58.4 18.0 %copy-start.17 = (bf16[2,128,768]{2,1,0:T(8,128)(2,1)S(1)}, bf16[2,128,768]{2,1,0:T(8,128)(2,1)}, u32[]{:S(2)}) copy-start(bf16[2,128,768]{2,1,0:T(8,128)(2,1)} %param.40) | copy-start | bytes 1179652
  78.3 123.4 %all-gather.17.cloned.1.call-start = ((), (), s32[]{:S(2)}) async-start(), calls=%async_computation.11 | async-start | bytes 6684672 | tf_op jit(solution)/shard_map/all_gather | solution.py:261
  79.2 260.4 %all-gather.11.cloned.1.call-start = ((), (), s32[]{:S(2)}) async-start(), calls=%async_computation.8 | async-start | bytes 1216512 | tf_op jit(solution)/shard_map/all_gather | solution.py:226
  79.7 261.8 %all-gather.13.cloned.1.call-start = ((), (), s32[]{:S(2)}) async-start(), calls=%async_computation.9 | async-start | bytes 4866048 | tf_op jit(solution)/shard_map/all_gather | solution.py:227
  80.3 306.7 %all-gather.15.cloned.1.call-start = ((), (), s32[]{:S(2)}) async-start(), calls=%async_computation.10 | async-start | bytes 4866048 | tf_op jit(solution)/shard_map/all_gather | solution.py:228
  80.9 1016.4 %reduce-scatter.9.cloned.1.call-start = ((), (), s32[]{:S(2)}) async-start(), calls=%async_computation.12 | async-start | bytes 13369344 | tf_op jit(solution)/shard_map/reduce_scatter | solution.py:344
  102.3 467.1 %copy-start.41 = (f32[768]{0:T(1024)}, f32[768]{0:T(1024)S(1)}, u32[]{:S(2)}) copy-start(f32[768]{0:T(1024)S(1)} %convert_element_type.263) | copy-start | bytes 9220
  102.3 453.1 %copy-start.43 = (f32[768]{0:T(1024)}, f32[768]{0:T(1024)S(1)}, u32[]{:S(2)}) copy-start(f32[768]{0:T(1024)S(1)} %convert_element_type.264) | copy-start | bytes 9220
  339.4 10.5 copy-start.48
  341.3 45.7 %copy-start.7 = (f32[128,768]{1,0:T(8,128)}, f32[128,768]{1,0:T(8,128)S(1)}, u32[]{:S(2)}) copy-start(f32[128,768]{1,0:T(8,128)S(1)} %get-tuple-element.1496) | copy-start | bytes 1179652
  341.3 228.1 %copy-start.49 = (f32[128]{0:T(128)}, f32[128]{0:T(128)S(1)}, u32[]{:S(2)}) copy-start(f32[128]{0:T(128)S(1)} %broadcast_multiply_fusion.1) | copy-start | bytes 1540
  341.5 227.9 %copy-start.53 = (f32[128]{0:T(128)}, f32[128]{0:T(128)S(1)}, u32[]{:S(2)}) copy-start(f32[128]{0:T(128)S(1)} %fusion.104) | copy-start | bytes 1540
  349.9 40.3 %copy-start.22 = (bf16[128,3072]{1,0:T(8,128)(2,1)}, bf16[128,3072]{1,0:T(8,128)(2,1)S(1)}, u32[]{:S(2)}) copy-start(bf16[128,3072]{1,0:T(8,128)(2,1)S(1)} %get-tuple-element.1442) | copy-start | bytes 2359300
  474.2 73.3 %copy-start.4 = (bf16[768,768]{1,0:T(8,128)(2,1)S(1)}, bf16[768,768]{1,0:T(8,128)(2,1)}, u32[]{:S(2)}) copy-start(bf16[768,768]{1,0:T(8,128)(2,1)} %all-gather.11.cloned.1.call-done) | copy-start | bytes 3538948
  549.0 20.4 %copy-start.5 = (f32[128,768]{1,0:T(8,128)}, f32[128,768]{1,0:T(8,128)S(1)}, u32[]{:S(2)}) copy-start(f32[128,768]{1,0:T(8,128)S(1)} %get-tuple-element.1491) | copy-start | bytes 1179652
  549.1 20.4 %copy-start.45 = (f32[128]{0:T(128)}, f32[128]{0:T(128)S(1)}, u32[]{:S(2)}) copy-start(f32[128]{0:T(128)S(1)} %broadcast_multiply_fusion.3) | copy-start | bytes 1540
  549.3 20.2 %copy-start.51 = (f32[128]{0:T(128)}, f32[128]{0:T(128)S(1)}, u32[]{:S(2)}) copy-start(f32[128]{0:T(128)S(1)} %fusion.102) | copy-start | bytes 1540
  584.2 81.2 %copy-start.62 = (f32[128]{0:T(128)S(1)}, f32[128]{0:T(128)}, u32[]{:S(2)}) copy-start(f32[128]{0:T(128)} %get-tuple-element.1432) | copy-start | bytes 1540
  668.0 10.9 copy-start.56
  678.9 120.9 %copy-start.63 = (pred[31]{0:T(512)(128)(4,1)S(1)}, pred[31]{0:T(512)(128)(4,1)}, u32[]{:S(2)}) copy-start(pred[31]{0:T(512)(128)(4,1)} %compare_and_fusion) | copy-start | bytes 97
  917.0 318.5 %reduce-scatter.11.cloned.1.call-start = ((), (), s32[]{:S(2)}) async-start(), calls=%async_computation.13 | async-start | bytes 13369344 | tf_op jit(solution)/shard_map/reduce_scatter | solution.py:344
  1004.3 336.0 %reduce-scatter.13.cloned.1.call-start = ((), (), s32[]{:S(2)}) async-start(), calls=%async_computation.14 | async-start | bytes 2433024 | tf_op jit(solution)/shard_map/reduce_scatter | solution.py:369
  1007.6 474.6 %reduce-scatter.15.cloned.1.call-start = ((), (), s32[]{:S(2)}) async-start(), calls=%async_computation.15 | async-start | bytes 9732096 | tf_op jit(solution)/shard_map/reduce_scatter | solution.py:370
  1015.5 608.3 %reduce-scatter.17.cloned.1.call-start = ((), (), s32[]{:S(2)}) async-start(), calls=%async_computation.16 | async-start | bytes 9732096 | tf_op jit(solution)/shard_map/reduce_scatter | solution.py:371
  1023.2 725.2 %reduce-scatter.19.cloned.1.call-start = ((), (), s32[]{:S(2)}) async-start(), calls=%async_computation.17 | async-start | bytes 7299072
  1023.5 213.2 %copy-start.34 = (bf16[128,768]{1,0:T(8,128)(2,1)}, bf16[128,768]{1,0:T(8,128)(2,1)S(1)}, u32[]{:S(2)}) copy-start(bf16[128,768]{1,0:T(8,128)(2,1)S(1)} %copy.96) | copy-start | bytes 589828
  1024.1 212.6 %copy-start.18 = (bf16[2,128,768]{2,1,0:T(8,128)(2,1)S(1)}, bf16[2,128,768]{2,1,0:T(8,128)(2,1)}, u32[]{:S(2)}) copy-start(bf16[2,128,768]{2,1,0:T(8,128)(2,1)} %param.40) | copy-start | bytes 1179652
  1024.5 213.4 %copy-start.28 = (bf16[128,768]{1,0:T(8,128)(2,1)}, bf16[128,768]{1,0:T(8,128)(2,1)S(1)}, u32[]{:S(2)}) copy-start(bf16[128,768]{1,0:T(8,128)(2,1)S(1)} %copy.100) | copy-start | bytes 589828
  1098.4 139.4 %copy-start.12 = (bf16[128,1536]{1,0:T(8,128)(2,1)}, bf16[128,1536]{1,0:T(8,128)(2,1)S(1)}, u32[]{:S(2)}) copy-start(bf16[128,1536]{1,0:T(8,128)(2,1)S(1)} %convert.16) | copy-start | bytes 1179652
  1250.0 68.1 %copy-start.1 = (bf16[768,2304]{1,0:T(8,128)(2,1)S(1)}, bf16[768,2304]{1,0:T(8,128)(2,1)}, u32[]{:S(2)}) copy-start(bf16[768,2304]{1,0:T(8,128)(2,1)} %all-gather.7.cloned.1.call-done) | copy-start | bytes 10616836
  (50 other events, 137.1 us)
Sparse Core Ops, SparseCore 0:
  10.9 62.6 all-gather.6
  78.4 60.2 all-gather.8
  141.5 60.0 all-gather.16
  204.4 52.5 all-gather.10
  259.8 62.4 all-gather.12
  325.0 61.9 all-gather.14
  917.2 180.0 reduce-scatter.8
  1101.3 134.1 reduce-scatter.10
  1241.4 98.8 reduce-scatter.12
  1346.6 135.5 reduce-scatter.14
  1488.7 135.0 reduce-scatter.16
  1629.9 118.4 reduce-scatter.18
where the time goes:
time: 1770 us; the launch traced here: 1760 us
  waiting for transfers between devices  789 us (45%)
  other arithmetic  329 us (19%)
  local copies, waits for them, and re-layouts  272 us (15%)
  loops' own time  131 us (7%)
  matrix products  114 us (6%)
  blocking collectives  105 us (6%)
    reduce_scatter x2, waiting for transfers between devices, local(): lax.psum_scatter(canvas, 'seq', scatter_dimension=0, tiled=True)  210 us
    reduce_scatter x1, waiting for transfers between devices, local(): lax.psum_scatter(totals[2], ('dp', 'seq'), scatter_dimension=0, tiled=True)  142 us
    reduce_scatter x1, waiting for transfers between devices, local(): lax.psum_scatter(totals[3], ('dp', 'seq'), scatter_dimension=0, tiled=True)  142 us
    eq x186, other arithmetic, block_mask(): return query_segment[:, None] == key_segments[block_index][None, :]  136 us
    unnamed x13, waiting for transfers between devices  127 us
    scatter-add x2, other arithmetic, local(): canvas.at[jnp.clip(block_ids, 0, seq_count - 1)]  111 us
    all_gather x2, waiting for transfers between devices, local(): lax.all_gather(jnp.concatenate([keys_now, values_now], axis=1), 'seq', ax...  98.8 us
    unnamed x2, blocking collectives  84.9 us
  transfers between devices with their start and end apart: 12, of which 10 were waited for; matrix products, arithmetic and copies ran while one was open for 15% of the time, Pallas kernels for 0%

commit v1 on v0

--- a/solution.py
+++ b/solution.py
@@ -1,6 +1,8 @@
 import jax
 import jax.numpy as jnp
 from jax import lax
+from jax.experimental import pallas as pl
+from jax.experimental.pallas import tpu as pltpu
 from jax.sharding import PartitionSpec as P
 
 HEADS = 12
@@ -176,7 +178,7 @@
     return jnp.sum(rows_low.astype(jnp.float32), axis=0)
 
 
-def local(
+def general_local(
     tokens,
     segments,
     qkv_weight,
@@ -398,6 +400,468 @@
     )
 
 
+CORE, XBIT, ZLOW, ZHIGH = 1, 2, 4, 8
+GROUPS = 4
+GROUP = HEADS // GROUPS * HEAD_DIM
+QROWS = 256
+
+
+def swap(value, bit):
+    return lax.ppermute(value, "seq", [(i, i ^ bit) for i in range(16)])
+
+
+def swap_rows(value):
+    return lax.ppermute(value, "dp", [(0, 1), (1, 0)])
+
+
+def pair(bit, own, other):
+    return jnp.where(bit == 0, own, other), jnp.where(bit == 0, other, own)
+
+
+def join(bit, own, other, axis):
+    return jnp.stack(pair(bit, own, other), axis=axis)
+
+
+def take(value, index, axis):
+    return lax.dynamic_index_in_dim(value, index, axis, keepdims=False)
+
+
+def head_lanes(head, width):
+    return lax.broadcasted_iota(jnp.int32, (1, width), 1) // HEAD_DIM == head
+
+
+def attend_kernel(q_ref, k_ref, v_ref, qseg_ref, kseg_ref, out_ref, log_ref):
+    width = q_ref.shape[1]
+    rows = q_ref.shape[0]
+    query = q_ref[...]
+    allowed = qseg_ref[...] == kseg_ref[...]
+
+    def visit(head, total):
+        lanes = head_lanes(head, width)
+        masked = jnp.where(lanes, query, jnp.zeros_like(query))
+        scores = lax.dot_general(
+            masked, k_ref[...], (((1,), (1,)), ((), ())), preferred_element_type=jnp.float32
+        )
+        scores = jnp.where(allowed, scores * 0.125, NEGATIVE)
+        top = jnp.max(scores, axis=1, keepdims=True)
+        expon = jnp.exp(scores - top)
+        norm = jnp.sum(expon, axis=1, keepdims=True)
+        value = jnp.dot(
+            expon.astype(jnp.bfloat16), v_ref[...], preferred_element_type=jnp.float32
+        )
+        log_rows = jnp.transpose(jnp.broadcast_to(top + jnp.log(norm), (rows, 128)))
+        log_ref[pl.ds(head, 1), :] = log_rows[0:1]
+        return total + jnp.where(lanes, value / norm, 0.0)
+
+    total = lax.fori_loop(0, width // HEAD_DIM, visit, jnp.zeros((rows, width), jnp.float32))
+    out_ref[...] = total.astype(jnp.bfloat16)
+
+
+def attend_group(query, keys, values, qseg_column, kseg_row):
+    rows, width = query.shape
+    count = keys.shape[0]
+    return pl.pallas_call(
+        attend_kernel,
+        grid=(rows // QROWS,),
+        in_specs=[
+            pl.BlockSpec((QROWS, width), lambda i: (i, 0)),
+            pl.BlockSpec((count, width), lambda i: (0, 0)),
+            pl.BlockSpec((count, width), lambda i: (0, 0)),
+            pl.BlockSpec((QROWS, 1), lambda i: (i, 0)),
+            pl.BlockSpec((1, count), lambda i: (0, 0)),
+        ],
+        out_specs=[
+            pl.BlockSpec((QROWS, width), lambda i: (i, 0)),
+            pl.BlockSpec((8, QROWS), lambda i: (0, i)),
+        ],
+        out_shape=[
+            jax.ShapeDtypeStruct((rows, width), jnp.bfloat16),
+            jax.ShapeDtypeStruct((8, rows), jnp.float32),
+        ],
+        cost_estimate=pl.CostEstimate(
+            flops=4 * rows * count * 256 * (width // HEAD_DIM),
+            bytes_accessed=4 * (rows + count) * width,
+            transcendentals=rows * count * (width // HEAD_DIM),
+        ),
+        compiler_params=pltpu.CompilerParams(vmem_limit_bytes=56 * 1024 * 1024),
+    )(query, keys, values, qseg_column, kseg_row)
+
+
+def attend_back_kernel(
+    q_ref, k_ref, v_ref, grad_ref, log_ref, qseg_ref, kseg_ref, dq_ref, dk_ref, dv_ref
+):
+    width = q_ref.shape[1]
+    query = q_ref[...]
+    grad = grad_ref[...]
+    allowed = kseg_ref[...] == qseg_ref[...]
+
+    @pl.when(pl.program_id(0) == 0)
+    def clear():
+        dk_ref[...] = jnp.zeros_like(dk_ref)
+        dv_ref[...] = jnp.zeros_like(dv_ref)
+
+    def visit(head, total):
+        lanes = head_lanes(head, width)
+        query_now = jnp.where(lanes, query, jnp.zeros_like(query))
+        grad_now = jnp.where(lanes, grad, jnp.zeros_like(grad))
+        scores = lax.dot_general(
+            k_ref[...], query_now, (((1,), (1,)), ((), ())), preferred_element_type=jnp.float32
+        )
+        prob = jnp.where(allowed, jnp.exp(scores * 0.125 - log_ref[pl.ds(head, 1), :]), 0.0)
+        grad_prob = lax.dot_general(
+            v_ref[...], grad_now, (((1,), (1,)), ((), ())), preferred_element_type=jnp.float32
+        )
+        delta = jnp.sum(prob * grad_prob, axis=0, keepdims=True)
+        grad_score = (prob * (grad_prob - delta)).astype(jnp.bfloat16)
+        dv_ref[...] += jnp.dot(
+            prob.astype(jnp.bfloat16), grad_now, preferred_element_type=jnp.float32
+        )
+        dk_ref[...] += 0.125 * jnp.dot(grad_score, query_now, preferred_element_type=jnp.float32)
+        dq = lax.dot_general(
+            grad_score, k_ref[...], (((0,), (0,)), ((), ())), preferred_element_type=jnp.float32
+        )
+        return total + jnp.where(lanes, dq * 0.125, 0.0)
+
+    total = lax.fori_loop(
+        0, width // HEAD_DIM, visit, jnp.zeros((q_ref.shape[0], width), jnp.float32)
+    )
+    dq_ref[...] = total.astype(jnp.bfloat16)
+
+
+def attend_group_back(query, keys, values, grad, log_total, qseg_row, kseg_column):
+    rows, width = query.shape
+    count = keys.shape[0]
+    return pl.pallas_call(
+        attend_back_kernel,
+        grid=(rows // QROWS,),
+        in_specs=[
+            pl.BlockSpec((QROWS, width), lambda i: (i, 0)),
+            pl.BlockSpec((count, width), lambda i: (0, 0)),
+            pl.BlockSpec((count, width), lambda i: (0, 0)),
+            pl.BlockSpec((QROWS, width), lambda i: (i, 0)),
+            pl.BlockSpec((8, QROWS), lambda i: (0, i)),
+            pl.BlockSpec((1, QROWS), lambda i: (0, i)),
+            pl.BlockSpec((count, 1), lambda i: (0, 0)),
+        ],
+        out_specs=[
+            pl.BlockSpec((QROWS, width), lambda i: (i, 0)),
+            pl.BlockSpec((count, width), lambda i: (0, 0)),
+            pl.BlockSpec((count, width), lambda i: (0, 0)),
+        ],
+        out_shape=[
+            jax.ShapeDtypeStruct((rows, width), jnp.bfloat16),
+            jax.ShapeDtypeStruct((count, width), jnp.float32),
+            jax.ShapeDtypeStruct((count, width), jnp.float32),
+        ],
+        cost_estimate=pl.CostEstimate(
+            flops=10 * rows * count * 256 * (width // HEAD_DIM),
+            bytes_accessed=8 * (rows + count) * width,
+            transcendentals=rows * count * (width // HEAD_DIM),
+        ),
+        compiler_params=pltpu.CompilerParams(vmem_limit_bytes=56 * 1024 * 1024),
+    )(query, keys, values, grad, log_total, qseg_row, kseg_column)
+
+
+def norm_parts(summed):
+    centred = summed - jnp.mean(summed, axis=-1, keepdims=True)
+    scale = lax.rsqrt(jnp.mean(centred * centred, axis=-1, keepdims=True) + EPS)
+    return centred * scale, scale
+
+
+def norm_back(grad, normal, scale, gain):
+    grad_normal = grad * gain
+    inside = grad_normal - jnp.mean(grad_normal, axis=-1, keepdims=True)
+    return scale * (inside - normal * jnp.mean(grad_normal * normal, axis=-1, keepdims=True))
+
+
+def gather_tokens(tokens, seq_mine):
+    first = jnp.concatenate(
+        [take(tokens, seq_mine, 0), swap(take(tokens, 1 - seq_mine, 0), ZHIGH)]
+    )
+    half = tokens.shape[-1] // 2
+    block = first.shape[0]
+    left, right = first[:, :half], first[:, half:]
+    left_two = jnp.concatenate([left, swap(left, XBIT)])
+    right_z = swap(right, ZLOW)
+    left_far = swap(left_two, ZLOW)
+    right_far = swap(jnp.concatenate([right, right_z]), XBIT)
+    right_four = jnp.concatenate([right, right_far[:block], right_z, right_far[block:]])
+    return jnp.concatenate([jnp.concatenate([left_two, left_far]), right_four], axis=1)
+
+
+def gather_segments(segments, seq_mine):
+    held = jnp.concatenate(
+        [take(segments, seq_mine, 0), swap(take(segments, 1 - seq_mine, 0), ZHIGH)]
+    ).reshape(1, -1)
+    held = jnp.concatenate([held, swap(held, XBIT)], axis=1)
+    held = jnp.concatenate([held, swap(held, ZLOW)], axis=1)
+    return jnp.concatenate([held, swap(held, CORE)], axis=1)
+
+
+def scatter_tokens(partial):
+    block = partial.shape[0] // 4
+    half = partial.shape[1] // 2
+    low = partial.astype(jnp.bfloat16)
+
+    def plus(one, other):
+        return one.astype(jnp.float32) + other.astype(jnp.float32)
+
+    left = plus(partial[: 2 * block, :half], swap(low[2 * block :, :half], ZLOW))
+    right_keep = jnp.concatenate(
+        [partial[:block, half:], partial[2 * block : 3 * block, half:]]
+    )
+    right_send = jnp.concatenate([low[block : 2 * block, half:], low[3 * block :, half:]])
+    right = plus(right_keep, swap(right_send, XBIT))
+    left = plus(left[:block], swap(left[block:].astype(jnp.bfloat16), XBIT))
+    right = plus(right[:block], swap(right[block:].astype(jnp.bfloat16), ZLOW))
+    both = jnp.concatenate([left, right], axis=1)
+    mine = block // 2
+    return both[:mine], swap(both[mine:].astype(jnp.bfloat16), ZHIGH).astype(jnp.float32)
+
+
+def gather_group_weight(weight, query_bias, value_bias, place):
+    dp_at, z_high, z_low, x_at, core = place
+    rows = weight.shape[0]
+    pieces = weight.reshape(rows, 3, 2, 2, GROUP).transpose(2, 3, 0, 1, 4)
+    pieces = pieces.reshape(2, 2, rows, 3 * GROUP)
+    biases = jnp.concatenate([query_bias, value_bias])
+    extra = jnp.pad(biases[None], ((0, 7), (0, 3 * GROUP - biases.shape[0])))
+    extra = jnp.broadcast_to(extra[None, None], (2, 2) + extra.shape)
+    pieces = jnp.concatenate([pieces, extra], axis=2)
+    held = join(x_at, take(pieces, x_at, 1), swap(take(pieces, 1 - x_at, 1), XBIT), 0)
+    held = join(z_low, take(held, z_low, 1), swap(take(held, 1 - z_low, 1), ZLOW), 0)
+    held = join(z_high, held, swap(held, ZHIGH), 0)
+    held = join(dp_at, held, swap_rows(held), 0)
+    held = join(core, held, swap(held, CORE), 4)
+    held = held.reshape(32, rows + 8, 3 * GROUP)
+    group = z_low * 2 + x_at
+    query_full = held[:, rows, :rows].reshape(-1)
+    value_full = held[:, rows, rows : 2 * rows].reshape(-1)
+    return (
+        held[:, :rows].reshape(32 * rows, 3 * GROUP),
+        take(query_full.reshape(GROUPS, GROUP), group, 0),
+        take(value_full.reshape(GROUPS, GROUP), group, 0),
+    )
+
+
+def scatter_group_weight(grad, query_sums, value_sums, place):
+    dp_at, z_high, z_low, x_at, core = place
+    rows = grad.shape[0] // 32
+    group = z_low * 2 + x_at
+    sums = jnp.concatenate([query_sums.reshape(8, rows), value_sums.reshape(8, rows)], axis=1)
+    owner = jnp.arange(32, dtype=jnp.int32)[:, None] // 8 == group
+    sums = jnp.where(owner, jnp.tile(sums, (4, 1)), 0.0)
+    extra = jnp.pad(sums[:, None], ((0, 0), (0, 7), (0, 3 * GROUP - 2 * rows)))
+    held = jnp.concatenate([grad.reshape(32, rows, 3 * GROUP), extra], axis=1)
+    held = held.astype(jnp.bfloat16)
+
+    def plus(one, other):
+        return (one.astype(jnp.float32) + other.astype(jnp.float32)).astype(jnp.bfloat16)
+
+    shape = held.shape[1:]
+    held = held.reshape((16, 2) + shape)
+    held = plus(take(held, core, 1), swap(take(held, 1 - core, 1), CORE))
+    held = held.reshape((2, 8) + shape)
+    held = plus(take(held, dp_at, 0), swap_rows(take(held, 1 - dp_at, 0)))
+    held = held.reshape((2, 4) + shape)
+    held = plus(take(held, z_high, 0), swap(take(held, 1 - z_high, 0), ZHIGH))
+    held = held.reshape((2, 2) + shape)
+    held = join(z_low, take(held, z_low, 0), swap(take(held, 1 - z_low, 0), ZLOW), 0)
+    held = join(x_at, take(held, x_at, 1), swap(take(held, 1 - x_at, 1), XBIT), 1)
+    held = held.reshape((GROUPS,) + shape).astype(jnp.float32)
+    weight = held[:, :rows].reshape(GROUPS, rows, 3, GROUP).transpose(1, 2, 0, 3)
+    biases = jnp.sum(held[:, rows, : 2 * rows], axis=0)
+    return weight.reshape(rows, 3 * GROUPS * GROUP), biases[:rows], biases[rows:]
+
+
+def heads_to_owners(attended, place):
+    _, _, z_low, x_at, _ = place
+    block = attended.shape[0] // 4
+    own = attended[:block]
+    x_part = swap(attended[block : 2 * block], XBIT)
+    z_part = swap(attended[2 * block : 3 * block], ZLOW)
+    far_part = swap(attended[3 * block :], XBIT | ZLOW)
+    near = jnp.concatenate(pair(x_at, own, x_part), axis=1)
+    far = jnp.concatenate(pair(x_at, z_part, far_part), axis=1)
+    rows = jnp.concatenate(pair(z_low, near, far), axis=1)
+    mine = block // 2
+    return jnp.concatenate([rows[:mine], swap(rows[mine:], ZHIGH)])
+
+
+def owners_to_heads(rows, place):
+    _, _, z_low, x_at, _ = place
+    mine = rows.shape[0] // 2
+    rows = jnp.concatenate([rows[:mine], swap(rows[mine:], ZHIGH)])
+    near, far = pair(z_low, rows[:, : 2 * GROUP], rows[:, 2 * GROUP :])
+    own, x_part = pair(x_at, near[:, :GROUP], near[:, GROUP:])
+    z_part, far_part = pair(x_at, far[:, :GROUP], far[:, GROUP:])
+    return jnp.concatenate(
+        [own, swap(x_part, XBIT), swap(z_part, ZLOW), swap(far_part, XBIT | ZLOW)]
+    )
+
+
+def local(
+    tokens,
+    segments,
+    qkv_weight,
+    out_weight,
+    up_weight,
+    down_weight,
+    query_bias,
+    value_bias,
+    out_bias,
+    first_gain,
+    first_shift,
+    up_bias,
+    down_bias,
+    second_gain,
+    second_shift,
+    cotangent,
+):
+    f32, low = jnp.float32, jnp.bfloat16
+    width = tokens.shape[-1]
+    shard = out_weight.shape[0]
+    up_chunks = up_weight.shape[1] // width
+    wide = up_chunks * shard
+    vectors = (out_bias, first_gain, first_shift, down_bias, second_gain, second_shift)
+    position = lax.axis_index("seq")
+    z_high, z_low = position // 8, position // 4 % 2
+    x_at, core = position // 2 % 2, position % 2
+    place = (lax.axis_index("dp"), z_high, z_low, x_at, core)
+    mine = z_high
+
+    up_parts = up_weight.reshape(shard, up_chunks, width).transpose(1, 0, 2).reshape(wide, width)
+    small = jnp.concatenate(vectors + (up_bias,))
+    small = jnp.pad(small[None], ((0, 7), (0, width - small.shape[0])))
+    packed = jnp.concatenate([out_weight, up_parts, down_weight, small])
+    gathered = lax.all_gather(packed, ("dp", "seq"), axis=0)
+
+    group_tokens = gather_tokens(tokens, mine)
+    all_segments = gather_segments(segments, mine)
+    group_weight, query_b, value_b = gather_group_weight(
+        qkv_weight, query_bias, value_bias, place
+    )
+    half = group_tokens.shape[0]
+    query = jnp.dot(group_tokens, group_weight[:, :GROUP], preferred_element_type=f32)
+    query = (query + query_b.astype(f32)).astype(low)
+    key_value = jnp.dot(group_tokens, group_weight[:, GROUP:], preferred_element_type=f32)
+    lift = jnp.concatenate([jnp.zeros((GROUP,), f32), value_b.astype(f32)])
+    key_value = (key_value + lift).astype(low)
+    key_value = jnp.concatenate([key_value, swap(key_value, CORE)])
+    keys, values = key_value[:, :GROUP], key_value[:, GROUP:]
+    segment_column = all_segments.reshape(-1, 1)
+    attended_group, log_total = attend_group(
+        query, keys, values, segment_column[:half], all_segments
+    )
+    attended = heads_to_owners(attended_group, place)
+
+    out_full = gathered[:, :shard].reshape(-1, width)
+    up_full = jnp.concatenate(
+        [
+            gathered[:, shard * (1 + at) : shard * (2 + at)].reshape(-1, width)
+            for at in range(up_chunks)
+        ],
+        axis=1,
+    )
+    down_full = gathered[:, shard + wide : shard + 2 * wide].reshape(-1, width)
+    flat = gathered[:, shard + 2 * wide].astype(f32)
+    out_b, first_g, first_s, down_b, second_g, second_s = (
+        flat[:, at * shard : (at + 1) * shard].reshape(-1) for at in range(len(vectors))
+    )
+    up_b = flat[:, 6 * shard : 6 * shard + wide].reshape(-1)
+
+    inputs = jnp.concatenate([take(tokens, mine, 0), take(tokens, 1 - mine, 0)])
+    branch = jnp.dot(attended, out_full, preferred_element_type=f32) + out_b
+    normal1, scale1 = norm_parts(inputs.astype(f32) + branch)
+    hidden = normal1 * first_g + first_s
+    hidden_low = hidden.astype(low)
+    inner = jnp.dot(hidden_low, up_full, preferred_element_type=f32) + up_b
+    activated, gelu_pull = jax.vjp(exact_gelu, inner)
+    activated_low = activated.astype(low)
+    second = jnp.dot(activated_low, down_full, preferred_element_type=f32) + down_b
+    normal2, scale2 = norm_parts(hidden + second)
+    output = (normal2 * second_g + second_s).astype(low)
+    output = jnp.stack(pair(mine, output[: output.shape[0] // 2], output[output.shape[0] // 2 :]))
+
+    upstream = jnp.concatenate([take(cotangent, mine, 0), take(cotangent, 1 - mine, 0)])
+    upstream = upstream.astype(f32)
+    grad_sum2 = norm_back(upstream, normal2, scale2, second_g)
+    grad_second = grad_sum2.astype(low)
+    (grad_inner,) = gelu_pull(data_grad(grad_second, down_full))
+    grad_inner = grad_inner.astype(low)
+    grad_hidden = grad_sum2 + data_grad(grad_inner, up_full)
+    grad_sum1 = norm_back(grad_hidden, normal1, scale1, first_g)
+    grad_branch = grad_sum1.astype(low)
+    grad_attended = data_grad(grad_branch, out_full).astype(low)
+
+    grad_out = weight_grad(attended, grad_branch).astype(low).reshape(32, shard, width)
+    grad_up = jnp.concatenate(
+        [
+            weight_grad(hidden_low, grad_inner[:, at * width : (at + 1) * width])
+            .astype(low)
+            .reshape(32, shard, width)
+            for at in range(up_chunks)
+        ],
+        axis=1,
+    )
+    grad_down = weight_grad(activated_low, grad_second).astype(low).reshape(32, wide, width)
+    sums = (
+        column_sum(grad_branch),
+        jnp.sum(grad_hidden * normal1, axis=0),
+        jnp.sum(grad_hidden, axis=0),
+        column_sum(grad_second),
+        jnp.sum(upstream * normal2, axis=0),
+        jnp.sum(upstream, axis=0),
+        column_sum(grad_inner),
+    )
+    sums = jnp.concatenate([item.reshape(32, -1) for item in sums], axis=1)
+    sums = jnp.pad(sums[:, None], ((0, 0), (0, 7), (0, width - sums.shape[1]))).astype(low)
+    partial = jnp.concatenate([grad_out, grad_up, grad_down, sums], axis=1)
+    reduced = lax.psum_scatter(
+        partial.reshape(-1, width), ("dp", "seq"), scatter_dimension=0, tiled=True
+    ).astype(f32)
+
+    grad_group = owners_to_heads(grad_attended, place)
+    grad_query, grad_keys, grad_values = attend_group_back(
+        query, keys, values, grad_group, log_total, all_segments[:, :half], segment_column
+    )
+    grad_kv = jnp.concatenate([grad_keys, grad_values], axis=1)
+    grad_kv = grad_kv[:half] + swap(grad_kv[half:].astype(low), CORE).astype(f32)
+    grad_merged = jnp.concatenate([grad_query, grad_kv.astype(low)], axis=1)
+    own_part, other_part = scatter_tokens(data_grad(grad_merged, group_weight))
+    count = own_part.shape[0]
+    own_grad = (grad_sum1[:count] + own_part).astype(low)
+    other_grad = (grad_sum1[count:] + other_part).astype(low)
+    input_grad = jnp.stack(pair(mine, own_grad, other_grad))
+    grad_qkv, grad_query_bias, grad_value_bias = scatter_group_weight(
+        weight_grad(group_tokens, grad_merged),
+        column_sum(grad_merged[:, :GROUP]),
+        column_sum(grad_merged[:, 2 * GROUP :]),
+        place,
+    )
+
+    up_rows = reduced[shard : shard + wide].reshape(up_chunks, shard, width)
+    tail = reduced[shard + 2 * wide]
+    parts = [tail[at * shard : (at + 1) * shard] for at in range(6)]
+    return (
+        output,
+        input_grad,
+        grad_qkv,
+        reduced[:shard],
+        up_rows.transpose(1, 0, 2).reshape(shard, -1),
+        reduced[shard + wide : shard + 2 * wide],
+        grad_query_bias,
+        grad_value_bias,
+        parts[0],
+        parts[1],
+        parts[2],
+        tail[6 * shard : 6 * shard + wide],
+        parts[3],
+        parts[4],
+        parts[5],
+    )
+
+
 def solution(mesh):
     in_specs = (
         P("dp", "seq", None),
@@ -434,4 +898,7 @@
         P(("dp", "seq")),
         P(("dp", "seq")),
     )
-    return jax.shard_map(local, mesh=mesh, in_specs=in_specs, out_specs=out_specs, check_vma=False)
+    fits = mesh.shape["dp"] == 2 and mesh.shape["seq"] == 16
+    return jax.shard_map(
+        local if fits else general_local, mesh=mesh, in_specs=in_specs, out_specs=out_specs, check_vma=False
+    )

time: 1770 us -> 358 us (0.20)
  waiting for transfers between devices: 789 us -> 124 us
  other arithmetic: 329 us -> 28.1 us
  local copies, waits for them, and re-layouts: 272 us -> 42.7 us
  loops' own time: 131 us -> 0 us
  blocking collectives: 105 us -> 0 us
  matrix products: 114 us -> 36.1 us
  Pallas kernels: 0 us -> 55.8 us
  starting transfers between devices: 0.74 us -> 49.2 us
    reduce_scatter x5 -> x1, waiting for transfers between devices: 511 us -> 13.2 us  [local(): lax.psum_scatter(partial.reshape(-1, width), ('dp', 'seq'), scatter_dimen...]
    all_gather x6 -> x1, waiting for transfers between devices: 151 us -> 0.01 us  [local(): gathered = lax.all_gather(packed, ('dp', 'seq'), axis=0)]
    eq x186 -> x1, other arithmetic: 136 us -> 0.01 us  [scatter_group_weight(): owner = jnp.arange(32, dtype=jnp.int32)[:, None] // 8 == group]
    another operation x192 -> x0, loops' own time: 131 us -> none  [the longest x2 42.4 us: attend_values(): lax.fori_loop(0, key_stack.shape[0], attend_visit, (zero_heads, zero_heads))]
    unnamed x13 -> x2, waiting for transfers between devices: 127 us -> 0.03 us
    scatter-add x2 -> x0, other arithmetic: 111 us -> none  [local(): canvas.at[jnp.clip(block_ids, 0, seq_count - 1)]]
    ppermute x0 -> x34, waiting for transfers between devices: none -> 111 us  [the longest x32 103 us: swap(): return lax.ppermute(value, 'seq', [(i, i ^ bit) for i in range(16)])]
    unnamed x2 -> x0, blocking collectives: 84.9 us -> none
  transfers between devices with their start and end apart: 12 -> 36, of which waited for: 10 -> 26; matrix products, arithmetic and copies ran while one was open for 15% -> 15% of each run, Pallas kernels for 0% -> 16%
where the time goes in v1:
time: 358 us; the launch traced here: 351 us
  waiting for transfers between devices  124 us (35%)
  Pallas kernels  55.8 us (16%)
  starting transfers between devices  49.2 us (14%)
  local copies, waits for them, and re-layouts  42.7 us (12%)
  matrix products  36.1 us (10%)
  other arithmetic  28.1 us (8%)
  between operations  15.4 us (4%)
    ppermute x32, waiting for transfers between devices, swap(): return lax.ppermute(value, 'seq', [(i, i ^ bit) for i in range(16)])  103 us
    ppermute x32, starting transfers between devices, swap(): return lax.ppermute(value, 'seq', [(i, i ^ bit) for i in range(16)])  46 us
    pallas_call x1, Pallas kernels, attend_group_back(): pl.pallas_call(attend_back_kernel, grid=(rows // QROWS,), in_specs=[pl.Bl...  32.1 us
    pallas_call x1, Pallas kernels, attend_group(): pl.pallas_call(attend_kernel, grid=(rows // QROWS,), in_specs=[pl.BlockSp...  23.7 us
    dot_general x7, matrix products, weight_grad(): jnp.einsum('rk,rn->kn', left_rows, right_rows, preferred_element_type=jnp...  14.1 us
    reduce_scatter x1, waiting for transfers between devices, local(): lax.psum_scatter(partial.reshape(-1, width), ('dp', 'seq'), scatter_dimen...  13.2 us
    dot_general x4, matrix products, data_grad(): jnp.einsum('rn,kn->rk', grad_rows, weight_full, preferred_element_type=jn...  9.85 us
    unnamed x60, local copies, waits for them, and re-layouts  9.6 us
  transfers between devices with their start and end apart: 36, of which 26 were waited for; matrix products, arithmetic and copies ran while one was open for 15% of the time, Pallas kernels for 16%

profile of v1, /device:TPU:0, one launch (start us, length us, event | category | flops | bytes accessed | tf_op | source)
XLA Modules:
  0.0 351.4 jit_solution(10890344292451713006)
XLA Ops:
  7.2 4.8 %concatenate.135 = bf16[240]{0:T(256)(128)(2,1)S(1)} concatenate(bf16[24]{0:T(256)(128)(2,1)} %param.24, bf16[24]{0:T(256)(128)(2,1)} %param.25, bf16[24]{0:T(256)(128)(2,1)} %param.26, bf16[24]{0:T(256)(128)(2,1)} %param.28, bf16[24]{0:T(256)(128)(2,1)} %param.29, bf16[24]{0:T(256)(128)(2,1)} %param.30, bf16[96]{0:T(256)(128)(2,1)} %param.27), dimensions={0} | concatenate | bytes 960 | tf_op jit(solution)/shard_map/concatenate | solution.py:734
  16.9 3.0 collective-permute-start.5
  24.6 2.7 collective-permute-start
  27.7 3.3 collective-permute-start.7
  31.0 14.3 %collective-permute-done = bf16[128,768]{1,0:T(8,128)(2,1)S(1)} collective-permute-done((bf16[128,768]{1,0:T(8,128)(2,1)S(1)}, bf16[128,768]{1,0:T(8,128)(2,1)S(1)}, u32[]{:S(2)}, u32[]{:S(2)}) %collective-permute-start) | collective-permute-done | bytes 196640 | tf_op jit(solution)/shard_map/ppermute | solution.py:410
  51.2 2.8 collective-permute-start.11
  55.9 7.5 %collective-permute-done.8 = bf16[2,2,2,32,576]{4,3,2,1,0:T(8,128)(2,1)S(1)} collective-permute-done((bf16[2,2,2,32,576]{4,3,2,1,0:T(8,128)(2,1)S(1)}, bf16[2,2,2,32,576]{4,3,2,1,0:T(8,128)(2,1)S(1)}, u32[]{:S(2)}, u32[]{:S(2)}) %collective-permute-start.8) | collective-permute-done | bytes 294944 | tf_op jit(solution)/shard_map/ppermute | solution.py:414
  65.3 7.6 %collective-permute-done.4 = bf16[512,384]{1,0:T(8,128)(2,1)S(1)} collective-permute-done((bf16[512,384]{1,0:T(8,128)(2,1)S(1)}, bf16[512,384]{1,0:T(8,128)(2,1)S(1)}, u32[]{:S(2)}, u32[]{:S(2)}) %collective-permute-start.4) | collective-permute-done | bytes 393248 | tf_op jit(solution)/shard_map/ppermute | solution.py:410
  75.5 3.3 collective-permute-done.13
  82.0 3.1 pad_maximum_fusion.4
  85.1 23.7 %shard_map.271 = (bf16[1024,192]{1,0:T(8,128)(2,1)}, f32[8,1024]{1,0:T(8,128)}) custom-call(bf16[1024,192]{1,0:T(8,128)(2,1)} %fusion.11.q_ref, bf16[2048,192]{1,0:T(8,128)(2,1)} %get-tuple-element.54.k_ref, bf16[2048,192]{1,0:T(8,128)(2,1)} %get-tuple-element.53.v_ref, s32[1024,1]{1,0:T(8,128)} %copy.52.qseg_ref, s32[1,2048]{1,0:T(1,128)} %pad_add_fusion.kseg_ref), custom_call_target="tpu_custom_call" | custom-call | flops 6442450944 | bytes 2359296 | tf_op jit(solution)/shard_map/pallas_call | solution.py:463
  111.2 4.3 %collective-permute-done.15 = bf16[256,192]{1,0:T(8,128)(2,1)S(1)} collective-permute-done((bf16[256,192]{1,0:T(8,128)(2,1)S(1)}, bf16[256,192]{1,0:T(8,128)(2,1)S(1)}, u32[]{:S(2)}, u32[]{:S(2)}) %collective-permute-start.15) | collective-permute-done | bytes 98336 | tf_op jit(solution)/shard_map/ppermute | solution.py:410
  119.8 4.1 %collective-permute-done.17 = bf16[256,192]{1,0:T(8,128)(2,1)S(1)} collective-permute-done((bf16[256,192]{1,0:T(8,128)(2,1)S(1)}, bf16[256,192]{1,0:T(8,128)(2,1)S(1)}, u32[]{:S(2)}, u32[]{:S(2)}) %collective-permute-start.17) | collective-permute-done | bytes 98336 | tf_op jit(solution)/shard_map/ppermute | solution.py:410
  125.7 5.2 %collective-permute-start.18 = (bf16[128,768]{1,0:T(8,128)(2,1)S(1)}, bf16[128,768]{1,0:T(8,128)(2,1)S(1)}, u32[]{:S(2)}, u32[]{:S(2)}) collective-permute-start(bf16[128,768]{1,0:T(8,128)(2,1)S(1)} %get-tuple-element.81), channel_id=1, source_target_pairs={{0,8},{1,9},{2,10},{3,11},{4,12},{5,13},{6,14},{7,15},{8,0},{9,1},... | collective-permute-start | bytes 589832 | tf_op jit(solution)/shard_map/ppermute | solution.py:410
  131.9 4.8 %slice.373 = bf16[32,96,768]{2,1,0:T(8,128)(2,1)} slice(bf16[32,224,768]{2,1,0:T(8,128)(2,1)} %bitcast.190), slice={[0:32], [120:216], [0:768]} | slice | bytes 9437184 | tf_op jit(solution)/shard_map/slice | solution.py:766
  136.7 5.0 %fusion.83 = (bf16[32,24,768]{2,1,0:T(8,128)(2,1)}, bf16[32,24,768]{2,1,0:T(8,128)(2,1)}, bf16[32,24,768]{2,1,0:T(8,128)(2,1)}, bf16[32,24,768]{2,1,0:T(8,128)(2,1)}, bf16[32,24,768]{2,1,0:T(8,128)(2,1)S(1)}) fusion(bf16[32,224,768]{2,1,0:T(8,128)(2,1)} %bitcast.191), kind=kLoop, calls=%fused_computation.266 | loop fusion | bytes 11796480 | tf_op jit(solution)/shard_map/slice | solution.py:761
  144.8 7.6 %multiply_convert_fusion = (bf16[256,3072]{1,0:T(8,128)(2,1)S(1)}, f32[256,3072]{1,0:T(8,128)S(1)}, f32[256,3072]{1,0:T(8,128)S(1)}) fusion(f32[3072]{0:T(1024)S(1)} %add.245, bf16[256,768]{1,0:T(8,128)(2,1)S(1)} %fusion.23, bf16[768,768]{1,0:T(8,128)(2,1)S(1)} %bitcast.219, bf16[768,768]{1,0:T(8,128)(2,1)S(1)} %bitcast.221, ...), kind=kOutput, calls=%fused_computation.8 | convolution fusion | flops 1278738432 | bytes 12988416 | tf_op jit(solution)/shard_map/dot_general | solution.py:778
  166.5 3.6 %convolution_convert_fusion = bf16[3072,768]{1,0:T(8,128)(2,1)} fusion(bf16[256,3072]{1,0:T(8,128)(2,1)S(1)} %get-tuple-element.42, f32[256,768]{1,0:T(8,128)S(1)} %get-tuple-element.37), kind=kOutput, calls=%fused_computation | convolution fusion | flops 1210515456 | bytes 7077888 | tf_op jit(solution)/shard_map/rk,rn->kn/dot_general | solution.py:170
  183.5 10.6 %collective-permute-done.19 = bf16[128,768]{1,0:T(8,128)(2,1)S(1)} collective-permute-done((bf16[128,768]{1,0:T(8,128)(2,1)S(1)}, bf16[128,768]{1,0:T(8,128)(2,1)S(1)}, u32[]{:S(2)}, u32[]{:S(2)}) %collective-permute-start.19) | collective-permute-done | bytes 196640 | tf_op jit(solution)/shard_map/ppermute | solution.py:410
  203.7 32.1 %shard_map.272 = (bf16[1024,192]{1,0:T(8,128)(2,1)}, f32[2048,192]{1,0:T(8,128)}, f32[2048,192]{1,0:T(8,128)}) custom-call(bf16[1024,192]{1,0:T(8,128)(2,1)} %fusion.11.q_ref, bf16[2048,192]{1,0:T(8,128)(2,1)} %get-tuple-element.54.k_ref, bf16[2048,192]{1,0:T(8,128)(2,1)} %get-tuple-element.53.v_ref, bf16[1024,192]{1,0:T(8,128)(2,1)} %pad_maximum_fusion.10.grad_ref, ...), custom_call_target="tpu_custom_call" | custom-call | flops 16106127360 | bytes 4718592 | tf_op jit(solution)/shard_map/pallas_call | solution.py:534
  235.8 2.9 fusion.9
  241.3 2.7 fusion.8
  245.4 4.7 %fusion.93 = (bf16[1024,768]{1,0:T(8,128)(2,1)S(1)}, f32[1024,768]{1,0:T(8,128)}) fusion(bf16[768,576]{1,0:T(8,128)(2,1)} %bitcast.209, bf16[1024,384]{1,0:T(8,128)(2,1)} %fusion.8, bf16[1024,192]{1,0:T(8,128)(2,1)S(1)} %copy-done.6), kind=kOutput, calls=%fused_computation.276 | convolution fusion | flops 909115392 | bytes 6782976 | tf_op jit(solution)/shard_map/rn,kn->rk/dot_general | solution.py:174
  252.8 2.8 convolution_convert_fusion.6
  258.0 5.8 %collective-permute-done.26 = bf16[512,384]{1,0:T(8,128)(2,1)} collective-permute-done((bf16[512,384]{1,0:T(8,128)(2,1)}, bf16[512,384]{1,0:T(8,128)(2,1)}, u32[]{:S(2)}, u32[]{:S(2)}) %collective-permute-start.26) | collective-permute-done | bytes 393248 | tf_op jit(solution)/shard_map/ppermute | solution.py:410
  265.0 9.1 %collective-permute-done.24 = bf16[512,384]{1,0:T(8,128)(2,1)S(1)} collective-permute-done((bf16[512,384]{1,0:T(8,128)(2,1)S(1)}, bf16[512,384]{1,0:T(8,128)(2,1)S(1)}, u32[]{:S(2)}, u32[]{:S(2)}) %collective-permute-start.24) | collective-permute-done | bytes 393248 | tf_op jit(solution)/shard_map/ppermute | solution.py:410
  279.1 3.1 collective-permute-done.25
  289.4 13.7 %collective-permute-done.28 = bf16[128,768]{1,0:T(8,128)(2,1)S(1)} collective-permute-done((bf16[128,768]{1,0:T(8,128)(2,1)S(1)}, bf16[128,768]{1,0:T(8,128)(2,1)S(1)}, u32[]{:S(2)}, u32[]{:S(2)}) %collective-permute-start.28) | collective-permute-done | bytes 196640 | tf_op jit(solution)/shard_map/ppermute | solution.py:410
  303.2 10.5 %collective-permute-done.31 = bf16[4,32,576]{2,1,0:T(8,128)(2,1)S(1)} collective-permute-done((bf16[4,32,576]{2,1,0:T(8,128)(2,1)S(1)}, bf16[4,32,576]{2,1,0:T(8,128)(2,1)S(1)}, u32[]{:S(2)}, u32[]{:S(2)}) %collective-permute-start.31) | collective-permute-done | bytes 147488 | tf_op jit(solution)/shard_map/ppermute | solution.py:410
  315.6 2.7 collective-permute-done.32
  319.4 3.4 collective-permute-done.33
  324.9 13.2 %reduce-scatter.2.cloned.1.call-done = bf16[224,768]{1,0:T(8,128)(2,1)} async-done(((bf16[7168,768]{1,0:T(8,128)(2,1)}), bf16[224,768]{1,0:T(8,128)(2,1)}) %reduce-scatter.2.cloned.1.call-update) | async-done | bytes 344080 | tf_op jit(solution)/shard_map/reduce_scatter | solution.py:820
  (264 shorter events, 108.2 us)
Async XLA Ops:
  7.2 123.7 %all-gather.3.cloned.1.call-start = ((), (), s32[]{:S(2)}) async-start(), calls=%async_computation.2 | async-start | bytes 11354112 | tf_op jit(solution)/shard_map/all_gather | solution.py:737
  14.7 323.4 %reduce-scatter.2.cloned.1.call-start = ((), (), s32[]{:S(2)}) async-start(), calls=%async_computation.1 | async-start | bytes 11354112 | tf_op jit(solution)/shard_map/reduce_scatter | solution.py:820
  16.9 5.5 %collective-permute-start.5 = (bf16[2,32,576]{2,1,0:T(8,128)(2,1)S(1)}, bf16[2,32,576]{2,1,0:T(8,128)(2,1)S(1)}, u32[]{:S(2)}, u32[]{:S(2)}) collective-permute-start(bf16[2,32,576]{2,1,0:T(8,128)(2,1)S(1)} %fusion.47), channel_id=1, source_target_pairs={{0,2},{1,3},{2,0},{3,1},{4,6},{5,7},{6,4},{7,5},{8,10},{9,11},{10,... | collective-permute-start | bytes 221192 | tf_op jit(solution)/shard_map/ppermute | solution.py:410
  22.4 5.3 %collective-permute-start.6 = (bf16[2,32,576]{2,1,0:T(8,128)(2,1)S(1)}, bf16[2,32,576]{2,1,0:T(8,128)(2,1)S(1)}, u32[]{:S(2)}, u32[]{:S(2)}) collective-permute-start(bf16[2,32,576]{2,1,0:T(8,128)(2,1)S(1)} %fusion.55), channel_id=1, source_target_pairs={{0,4},{1,5},{2,6},{3,7},{4,0},{5,1},{6,2},{7,3},{8,12},{9,13},{10,... | collective-permute-start | bytes 221192 | tf_op jit(solution)/shard_map/ppermute | solution.py:410
  24.6 20.7 %collective-permute-start = (bf16[128,768]{1,0:T(8,128)(2,1)S(1)}, bf16[128,768]{1,0:T(8,128)(2,1)S(1)}, u32[]{:S(2)}, u32[]{:S(2)}) collective-permute-start(bf16[128,768]{1,0:T(8,128)(2,1)S(1)} %get-tuple-element.86), channel_id=1, source_target_pairs={{0,8},{1,9},{2,10},{3,11},{4,12},{5,13},{6,14},{7,15},{8,0},{9,1},... | collective-permute-start | bytes 589832 | tf_op jit(solution)/shard_map/ppermute | solution.py:410
  27.7 21.7 %collective-permute-start.7 = (bf16[2,2,32,576]{3,2,1,0:T(8,128)(2,1)S(1)}, bf16[2,2,32,576]{3,2,1,0:T(8,128)(2,1)S(1)}, u32[]{:S(2)}, u32[]{:S(2)}) collective-permute-start(bf16[2,2,32,576]{3,2,1,0:T(8,128)(2,1)S(1)} %pad_maximum_fusion.28), channel_id=1, source_target_pairs={{0,8},{1,9},{2,10},{3,11},{4,12},{5,13},{6,14},{7,15},{8,0},{9,1},... | collective-permute-start | bytes 442376 | tf_op jit(solution)/shard_map/ppermute | solution.py:410
  45.4 8.7 %collective-permute-start.1 = (bf16[256,384]{1,0:T(8,128)(2,1)S(1)}, bf16[256,384]{1,0:T(8,128)(2,1)S(1)}, u32[]{:S(2)}, u32[]{:S(2)}) collective-permute-start(bf16[256,384]{1,0:T(8,128)(2,1)S(1)} %get-tuple-element.82), channel_id=1, source_target_pairs={{0,2},{1,3},{2,0},{3,1},{4,6},{5,7},{6,4},{7,5},{8,10},{9,11},{10,... | collective-permute-start | bytes 589832 | tf_op jit(solution)/shard_map/ppermute | solution.py:410
  46.9 7.4 %collective-permute-start.3 = (bf16[256,384]{1,0:T(8,128)(2,1)S(1)}, bf16[256,384]{1,0:T(8,128)(2,1)S(1)}, u32[]{:S(2)}, u32[]{:S(2)}) collective-permute-start(bf16[256,384]{1,0:T(8,128)(2,1)S(1)} %get-tuple-element.83), channel_id=1, source_target_pairs={{0,4},{1,5},{2,6},{3,7},{4,0},{5,1},{6,2},{7,3},{8,12},{9,13},{10,... | collective-permute-start | bytes 589832 | tf_op jit(solution)/shard_map/ppermute | solution.py:410
  49.6 13.8 %collective-permute-start.8 = (bf16[2,2,2,32,576]{4,3,2,1,0:T(8,128)(2,1)S(1)}, bf16[2,2,2,32,576]{4,3,2,1,0:T(8,128)(2,1)S(1)}, u32[]{:S(2)}, u32[]{:S(2)}) collective-permute-start(bf16[2,2,2,32,576]{4,3,2,1,0:T(8,128)(2,1)S(1)} %pad_maximum_fusion.20), channel_id=1, source_target_pairs={{0,16},{16,0},{1,17},{17,1},{2,18},{18,2},{3,19},{19,3},{4,20},{20... | collective-permute-start | bytes 884744 | tf_op jit(solution)/shard_map/ppermute | solution.py:414
  51.2 12.5 %collective-permute-start.11 = (s32[128]{0:T(128)S(1)}, s32[128]{0:T(128)S(1)}, u32[]{:S(2)}, u32[]{:S(2)}) collective-permute-start(s32[128]{0:T(128)S(1)} %get-tuple-element.113), channel_id=1, source_target_pairs={{0,8},{1,9},{2,10},{3,11},{4,12},{5,13},{6,14},{7,15},{8,0},{9,1},... | collective-permute-start | bytes 1544 | tf_op jit(solution)/shard_map/ppermute | solution.py:410
  54.1 18.9 %collective-permute-start.2 = (bf16[512,384]{1,0:T(8,128)(2,1)S(1)}, bf16[512,384]{1,0:T(8,128)(2,1)S(1)}, u32[]{:S(2)}, u32[]{:S(2)}) collective-permute-start(bf16[512,384]{1,0:T(8,128)(2,1)S(1)} %pad_maximum_fusion.13), channel_id=1, source_target_pairs={{0,4},{1,5},{2,6},{3,7},{4,0},{5,1},{6,2},{7,3},{8,12},{9,13},{10,... | collective-permute-start | bytes 1179656 | tf_op jit(solution)/shard_map/ppermute | solution.py:410
  54.4 18.5 %collective-permute-start.4 = (bf16[512,384]{1,0:T(8,128)(2,1)S(1)}, bf16[512,384]{1,0:T(8,128)(2,1)S(1)}, u32[]{:S(2)}, u32[]{:S(2)}) collective-permute-start(bf16[512,384]{1,0:T(8,128)(2,1)S(1)} %pad_maximum_fusion.14), channel_id=1, source_target_pairs={{0,2},{1,3},{2,0},{3,1},{4,6},{5,7},{6,4},{7,5},{8,10},{9,11},{10,... | collective-permute-start | bytes 1179656 | tf_op jit(solution)/shard_map/ppermute | solution.py:410
  63.6 9.5 %collective-permute-start.9 = (bf16[2,2,2,2,32,576]{5,4,3,2,1,0:T(8,128)(2,1)S(1)}, bf16[2,2,2,2,32,576]{5,4,3,2,1,0:T(8,128)(2,1)S(1)}, u32[]{:S(2)}, u32[]{:S(2)}) collective-permute-start(bf16[2,2,2,2,32,576]{5,4,3,2,1,0:T(8,128)(2,1)S(1)} %pad_maximum_fusion.9), channel_id=1, source_target_pairs={{0,1},{1,0},{2,3},{3,2},{4,5},{5,4},{6,7},{7,6},{8,9},{9,8},{10,11... | collective-permute-start | bytes 1769480 | tf_op jit(solution)/shard_map/ppermute | solution.py:410
  63.7 11.4 %collective-permute-start.12 = (s32[1,256]{1,0:T(1,128)S(1)}, s32[1,256]{1,0:T(1,128)S(1)}, u32[]{:S(2)}, u32[]{:S(2)}) collective-permute-start(s32[1,256]{1,0:T(1,128)S(1)} %bitcast.235), channel_id=1, source_target_pairs={{0,2},{1,3},{2,0},{3,1},{4,6},{5,7},{6,4},{7,5},{8,10},{9,11},{10,... | collective-permute-start | bytes 3080 | tf_op jit(solution)/shard_map/ppermute | solution.py:410
  75.1 7.0 %collective-permute-start.10 = (bf16[1024,384]{1,0:T(8,128)(2,1)S(1)}, bf16[1024,384]{1,0:T(8,128)(2,1)}, u32[]{:S(2)}, u32[]{:S(2)}) collective-permute-start(bf16[1024,384]{1,0:T(8,128)(2,1)S(1)} %add_convert_fusion.1), channel_id=1, source_target_pairs={{0,1},{1,0},{2,3},{3,2},{4,5},{5,4},{6,7},{7,6},{8,9},{9,8},{10,11... | collective-permute-start | bytes 2359304 | tf_op jit(solution)/shard_map/ppermute | solution.py:410
  109.8 5.8 %collective-permute-start.15 = (bf16[256,192]{1,0:T(8,128)(2,1)S(1)}, bf16[256,192]{1,0:T(8,128)(2,1)S(1)}, u32[]{:S(2)}, u32[]{:S(2)}) collective-permute-start(bf16[256,192]{1,0:T(8,128)(2,1)S(1)} %slice.279), channel_id=1, source_target_pairs={{0,2},{1,3},{2,0},{3,1},{4,6},{5,7},{6,4},{7,5},{8,10},{9,11},{10,... | collective-permute-start | bytes 294920 | tf_op jit(solution)/shard_map/ppermute | solution.py:410
  116.6 7.3 %collective-permute-start.17 = (bf16[256,192]{1,0:T(8,128)(2,1)S(1)}, bf16[256,192]{1,0:T(8,128)(2,1)S(1)}, u32[]{:S(2)}, u32[]{:S(2)}) collective-permute-start(bf16[256,192]{1,0:T(8,128)(2,1)S(1)} %get-tuple-element.70), channel_id=1, source_target_pairs={{0,6},{1,7},{2,4},{3,5},{4,2},{5,3},{6,0},{7,1},{8,14},{9,15},{10,... | collective-permute-start | bytes 294920 | tf_op jit(solution)/shard_map/ppermute | solution.py:410
  118.6 6.8 %collective-permute-start.16 = (bf16[256,192]{1,0:T(8,128)(2,1)S(1)}, bf16[256,192]{1,0:T(8,128)(2,1)S(1)}, u32[]{:S(2)}, u32[]{:S(2)}) collective-permute-start(bf16[256,192]{1,0:T(8,128)(2,1)S(1)} %get-tuple-element.71), channel_id=1, source_target_pairs={{0,4},{1,5},{2,6},{3,7},{4,0},{5,1},{6,2},{7,3},{8,12},{9,13},{10,... | collective-permute-start | bytes 294920 | tf_op jit(solution)/shard_map/ppermute | solution.py:410
  125.7 16.8 %collective-permute-start.18 = (bf16[128,768]{1,0:T(8,128)(2,1)S(1)}, bf16[128,768]{1,0:T(8,128)(2,1)S(1)}, u32[]{:S(2)}, u32[]{:S(2)}) collective-permute-start(bf16[128,768]{1,0:T(8,128)(2,1)S(1)} %get-tuple-element.81), channel_id=1, source_target_pairs={{0,8},{1,9},{2,10},{3,11},{4,12},{5,13},{6,14},{7,15},{8,0},{9,1},... | collective-permute-start | bytes 589832 | tf_op jit(solution)/shard_map/ppermute | solution.py:410
  183.4 10.7 %collective-permute-start.19 = (bf16[128,768]{1,0:T(8,128)(2,1)S(1)}, bf16[128,768]{1,0:T(8,128)(2,1)S(1)}, u32[]{:S(2)}, u32[]{:S(2)}) collective-permute-start(bf16[128,768]{1,0:T(8,128)(2,1)S(1)} %get-tuple-element.77), channel_id=1, source_target_pairs={{0,8},{1,9},{2,10},{3,11},{4,12},{5,13},{6,14},{7,15},{8,0},{9,1},... | collective-permute-start | bytes 589832 | tf_op jit(solution)/shard_map/ppermute | solution.py:410
  194.3 6.4 %collective-permute-start.20 = (bf16[256,192]{1,0:T(8,128)(2,1)S(1)}, bf16[256,192]{1,0:T(8,128)(2,1)S(1)}, u32[]{:S(2)}, u32[]{:S(2)}) collective-permute-start(bf16[256,192]{1,0:T(8,128)(2,1)S(1)} %get-tuple-element.103), channel_id=1, source_target_pairs={{0,2},{1,3},{2,0},{3,1},{4,6},{5,7},{6,4},{7,5},{8,10},{9,11},{10,... | collective-permute-start | bytes 294920 | tf_op jit(solution)/shard_map/ppermute | solution.py:410
  195.7 5.8 %collective-permute-start.21 = (bf16[256,192]{1,0:T(8,128)(2,1)S(1)}, bf16[256,192]{1,0:T(8,128)(2,1)S(1)}, u32[]{:S(2)}, u32[]{:S(2)}) collective-permute-start(bf16[256,192]{1,0:T(8,128)(2,1)S(1)} %get-tuple-element.104), channel_id=1, source_target_pairs={{0,4},{1,5},{2,6},{3,7},{4,0},{5,1},{6,2},{7,3},{8,12},{9,13},{10,... | collective-permute-start | bytes 294920 | tf_op jit(solution)/shard_map/ppermute | solution.py:410
  195.8 7.0 %collective-permute-start.22 = (bf16[256,192]{1,0:T(8,128)(2,1)S(1)}, bf16[256,192]{1,0:T(8,128)(2,1)S(1)}, u32[]{:S(2)}, u32[]{:S(2)}) collective-permute-start(bf16[256,192]{1,0:T(8,128)(2,1)S(1)} %get-tuple-element.105), channel_id=1, source_target_pairs={{0,6},{1,7},{2,4},{3,5},{4,2},{5,3},{6,0},{7,1},{8,14},{9,15},{10,... | collective-permute-start | bytes 294920 | tf_op jit(solution)/shard_map/ppermute | solution.py:410
  251.0 12.9 %collective-permute-start.26 = (bf16[512,384]{1,0:T(8,128)(2,1)}, bf16[512,384]{1,0:T(8,128)(2,1)}, u32[]{:S(2)}, u32[]{:S(2)}) collective-permute-start(bf16[512,384]{1,0:T(8,128)(2,1)} %pad_maximum_fusion.18), channel_id=1, source_target_pairs={{0,2},{1,3},{2,0},{3,1},{4,6},{5,7},{6,4},{7,5},{8,10},{9,11},{10,... | collective-permute-start | bytes 1179656 | tf_op jit(solution)/shard_map/ppermute | solution.py:410
  256.4 20.9 %collective-permute-start.29 = (bf16[16,32,576]{2,1,0:T(8,128)(2,1)S(1)}, bf16[16,32,576]{2,1,0:T(8,128)(2,1)S(1)}, u32[]{:S(2)}, u32[]{:S(2)}) collective-permute-start(bf16[16,32,576]{2,1,0:T(8,128)(2,1)S(1)} %fusion.26), channel_id=1, source_target_pairs={{0,1},{1,0},{2,3},{3,2},{4,5},{5,4},{6,7},{7,6},{8,9},{9,8},{10,11... | collective-permute-start | bytes 1769480 | tf_op jit(solution)/shard_map/ppermute | solution.py:410
  256.5 17.5 %collective-permute-start.24 = (bf16[512,384]{1,0:T(8,128)(2,1)S(1)}, bf16[512,384]{1,0:T(8,128)(2,1)S(1)}, u32[]{:S(2)}, u32[]{:S(2)}) collective-permute-start(bf16[512,384]{1,0:T(8,128)(2,1)S(1)} %slice.391), channel_id=1, source_target_pairs={{0,4},{1,5},{2,6},{3,7},{4,0},{5,1},{6,2},{7,3},{8,12},{9,13},{10,... | collective-permute-start | bytes 1179656 | tf_op jit(solution)/shard_map/ppermute | solution.py:410
  275.3 7.0 %collective-permute-start.25 = (bf16[256,384]{1,0:T(8,128)(2,1)S(1)}, bf16[256,384]{1,0:T(8,128)(2,1)S(1)}, u32[]{:S(2)}, u32[]{:S(2)}) collective-permute-start(bf16[256,384]{1,0:T(8,128)(2,1)S(1)} %slice.523), channel_id=1, source_target_pairs={{0,2},{1,3},{2,0},{3,1},{4,6},{5,7},{6,4},{7,5},{8,10},{9,11},{10,... | collective-permute-start | bytes 589832 | tf_op jit(solution)/shard_map/ppermute | solution.py:410
  276.8 6.7 %collective-permute-start.27 = (bf16[256,384]{1,0:T(8,128)(2,1)S(1)}, bf16[256,384]{1,0:T(8,128)(2,1)S(1)}, u32[]{:S(2)}, u32[]{:S(2)}) collective-permute-start(bf16[256,384]{1,0:T(8,128)(2,1)S(1)} %slice.522), channel_id=1, source_target_pairs={{0,4},{1,5},{2,6},{3,7},{4,0},{5,1},{6,2},{7,3},{8,12},{9,13},{10,... | collective-permute-start | bytes 589832 | tf_op jit(solution)/shard_map/ppermute | solution.py:410
  277.6 9.2 %collective-permute-start.30 = (bf16[8,32,576]{2,1,0:T(8,128)(2,1)S(1)}, bf16[8,32,576]{2,1,0:T(8,128)(2,1)S(1)}, u32[]{:S(2)}, u32[]{:S(2)}) collective-permute-start(bf16[8,32,576]{2,1,0:T(8,128)(2,1)S(1)} %dynamic-slice_bitcast_fusion), channel_id=1, source_target_pairs={{0,16},{16,0},{1,17},{17,1},{2,18},{18,2},{3,19},{19,3},{4,20},{20... | collective-permute-start | bytes 884744 | tf_op jit(solution)/shard_map/ppermute | solution.py:414
  283.5 19.6 %collective-permute-start.28 = (bf16[128,768]{1,0:T(8,128)(2,1)S(1)}, bf16[128,768]{1,0:T(8,128)(2,1)S(1)}, u32[]{:S(2)}, u32[]{:S(2)}) collective-permute-start(bf16[128,768]{1,0:T(8,128)(2,1)S(1)} %fusion.38), channel_id=1, source_target_pairs={{0,8},{1,9},{2,10},{3,11},{4,12},{5,13},{6,14},{7,15},{8,0},{9,1},... | collective-permute-start | bytes 589832 | tf_op jit(solution)/shard_map/ppermute | solution.py:410
  286.9 26.8 %collective-permute-start.31 = (bf16[4,32,576]{2,1,0:T(8,128)(2,1)S(1)}, bf16[4,32,576]{2,1,0:T(8,128)(2,1)S(1)}, u32[]{:S(2)}, u32[]{:S(2)}) collective-permute-start(bf16[4,32,576]{2,1,0:T(8,128)(2,1)S(1)} %dynamic-slice_bitcast_fusion.5), channel_id=1, source_target_pairs={{0,8},{1,9},{2,10},{3,11},{4,12},{5,13},{6,14},{7,15},{8,0},{9,1},... | collective-permute-start | bytes 442376 | tf_op jit(solution)/shard_map/ppermute | solution.py:410
  313.8 4.5 %collective-permute-start.32 = (bf16[2,32,576]{2,1,0:T(8,128)(2,1)S(1)}, bf16[2,32,576]{2,1,0:T(8,128)(2,1)S(1)}, u32[]{:S(2)}, u32[]{:S(2)}) collective-permute-start(bf16[2,32,576]{2,1,0:T(8,128)(2,1)S(1)} %dynamic-slice_bitcast_fusion.6), channel_id=1, source_target_pairs={{0,4},{1,5},{2,6},{3,7},{4,0},{5,1},{6,2},{7,3},{8,12},{9,13},{10,... | collective-permute-start | bytes 221192 | tf_op jit(solution)/shard_map/ppermute | solution.py:410
  (30 other events, 265.8 us)
Sparse Core Ops, SparseCore 0:
  14.8 105.9 all-gather.2
  183.0 154.9 reduce-scatter.1

commit v2 on v1

--- a/solution.py
+++ b/solution.py
@@ -598,25 +598,36 @@
     return jnp.concatenate([held, swap(held, CORE)], axis=1)
 
 
-def scatter_tokens(partial):
+def add_pair(one, other):
+    return one.astype(jnp.float32) + other.astype(jnp.float32)
+
+
+def scatter_first(partial):
     block = partial.shape[0] // 4
     half = partial.shape[1] // 2
     low = partial.astype(jnp.bfloat16)
-
-    def plus(one, other):
-        return one.astype(jnp.float32) + other.astype(jnp.float32)
-
-    left = plus(partial[: 2 * block, :half], swap(low[2 * block :, :half], ZLOW))
-    right_keep = jnp.concatenate(
-        [partial[:block, half:], partial[2 * block : 3 * block, half:]]
-    )
-    right_send = jnp.concatenate([low[block : 2 * block, half:], low[3 * block :, half:]])
-    right = plus(right_keep, swap(right_send, XBIT))
-    left = plus(left[:block], swap(left[block:].astype(jnp.bfloat16), XBIT))
-    right = plus(right[:block], swap(right[block:].astype(jnp.bfloat16), ZLOW))
-    both = jnp.concatenate([left, right], axis=1)
-    mine = block // 2
-    return both[:mine], swap(both[mine:].astype(jnp.bfloat16), ZHIGH).astype(jnp.float32)
+    left = swap(low[2 * block :, :half], ZLOW)
+    right = jnp.concatenate([low[block : 2 * block, half:], low[3 * block :, half:]])
+    return left, swap(right, XBIT)
+
+
+def scatter_second(partial, left_got, right_got):
+    block = partial.shape[0] // 4
+    half = partial.shape[1] // 2
+    left = add_pair(partial[: 2 * block, :half], left_got)
+    right = jnp.concatenate([partial[:block, half:], partial[2 * block : 3 * block, half:]])
+    right = add_pair(right, right_got)
+    got = (
+        swap(left[block:].astype(jnp.bfloat16), XBIT),
+        swap(right[block:].astype(jnp.bfloat16), ZLOW),
+    )
+    return left[:block], right[:block], got
+
+
+def scatter_third(left, right, got):
+    both = jnp.concatenate([add_pair(left, got[0]), add_pair(right, got[1])], axis=1)
+    mine = both.shape[0] // 2
+    return both[:mine], swap(both[mine:].astype(jnp.bfloat16), ZHIGH)
 
 
 def gather_group_weight(weight, query_bias, value_bias, place):
@@ -672,6 +683,33 @@
     weight = held[:, :rows].reshape(GROUPS, rows, 3, GROUP).transpose(1, 2, 0, 3)
     biases = jnp.sum(held[:, rows, : 2 * rows], axis=0)
     return weight.reshape(rows, 3 * GROUPS * GROUP), biases[:rows], biases[rows:]
+
+
+class Chain:
+    def __init__(self, held, place):
+        self.place = place
+        self.left = list(range(5))
+        self.held = held.reshape((2, 2, 2, 2, 2) + held.shape[1:])
+
+    def send(self, step):
+        self.step, self.axis = step, self.left.index(step)
+        sent = take(self.held, 1 - self.place[step], self.axis)
+        bits = (None, ZHIGH, ZLOW, XBIT, CORE)
+        self.got = swap(sent, bits[step]) if step else swap_rows(sent)
+
+    def add(self):
+        self.left.remove(self.step)
+        kept = take(self.held, self.place[self.step], self.axis).astype(jnp.float32)
+        kept = kept + self.got.astype(jnp.float32)
+        self.held = kept.astype(jnp.bfloat16) if self.left else kept
+
+
+def meet(values, chains):
+    values, got = lax.optimization_barrier((values, [chain.got for chain in chains]))
+    for chain, arrived in zip(chains, got):
+        chain.got = arrived
+        chain.add()
+    return values
 
 
 def heads_to_owners(attended, place):
@@ -731,8 +769,10 @@
     mine = z_high
 
     up_parts = up_weight.reshape(shard, up_chunks, width).transpose(1, 0, 2).reshape(wide, width)
-    small = jnp.concatenate(vectors + (up_bias,))
-    small = jnp.pad(small[None], ((0, 7), (0, width - small.shape[0])))
+    small, start = jnp.zeros((8, width), low), 0
+    for vector in vectors + (up_bias,):
+        ends = (start, width - start - vector.shape[0])
+        small, start = small + jnp.pad(vector[None], ((0, 7), ends)), start + vector.shape[0]
     packed = jnp.concatenate([out_weight, up_parts, down_weight, small])
     gathered = lax.all_gather(packed, ("dp", "seq"), axis=0)
 
@@ -794,17 +834,9 @@
     grad_branch = grad_sum1.astype(low)
     grad_attended = data_grad(grad_branch, out_full).astype(low)
 
-    grad_out = weight_grad(attended, grad_branch).astype(low).reshape(32, shard, width)
-    grad_up = jnp.concatenate(
-        [
-            weight_grad(hidden_low, grad_inner[:, at * width : (at + 1) * width])
-            .astype(low)
-            .reshape(32, shard, width)
-            for at in range(up_chunks)
-        ],
-        axis=1,
-    )
-    grad_down = weight_grad(activated_low, grad_second).astype(low).reshape(32, wide, width)
+    grad_down = weight_grad(activated_low, grad_second).astype(low)
+    grad_up = weight_grad(hidden_low, grad_inner).astype(low)
+    grad_out = weight_grad(attended, grad_branch).astype(low)
     sums = (
         column_sum(grad_branch),
         jnp.sum(grad_hidden * normal1, axis=0),
@@ -816,19 +848,42 @@
     )
     sums = jnp.concatenate([item.reshape(32, -1) for item in sums], axis=1)
     sums = jnp.pad(sums[:, None], ((0, 0), (0, 7), (0, width - sums.shape[1]))).astype(low)
-    partial = jnp.concatenate([grad_out, grad_up, grad_down, sums], axis=1)
-    reduced = lax.psum_scatter(
-        partial.reshape(-1, width), ("dp", "seq"), scatter_dimension=0, tiled=True
-    ).astype(f32)
+    rest = jnp.concatenate([grad_out.reshape(32, shard, width), sums], axis=1)
+    at_dp, at_high, at_low, at_x, at_core = range(5)
+    down = Chain(grad_down.reshape(32, wide, width), place)
+    up = Chain(grad_up.reshape(32, shard, -1), place)
+    rest = Chain(rest, place)
+    chains = (down, up, rest)
+    for chain in chains:
+        chain.send(at_core)
 
     grad_group = owners_to_heads(grad_attended, place)
-    grad_query, grad_keys, grad_values = attend_group_back(
+    grad_group = meet(grad_group, chains)
+    down.send(at_x)
+    up.send(at_dp)
+    rest.send(at_low)
+    attention = attend_group_back(
         query, keys, values, grad_group, log_total, all_segments[:, :half], segment_column
     )
+    grad_query, grad_keys, grad_values = meet(attention, chains)
+    down.send(at_dp)
+    up.send(at_x)
+    rest.send(at_x)
     grad_kv = jnp.concatenate([grad_keys, grad_values], axis=1)
     grad_kv = grad_kv[:half] + swap(grad_kv[half:].astype(low), CORE).astype(f32)
     grad_merged = jnp.concatenate([grad_query, grad_kv.astype(low)], axis=1)
-    own_part, other_part = scatter_tokens(data_grad(grad_merged, group_weight))
+    back = data_grad(grad_merged, group_weight)
+    left_got, right_got = meet(scatter_first(back), chains)
+    down.send(at_low)
+    up.send(at_low)
+    rest.send(at_dp)
+    left, right, got = scatter_second(back, left_got, right_got)
+    left, right, got = meet((left, right, got), chains)
+    for chain in chains:
+        chain.send(at_high)
+    own_part, other_part = scatter_third(left, right, got)
+    other_part = meet(other_part, chains).astype(f32)
+    down_mine, up_mine, rest_mine = (chain.held for chain in chains)
     count = own_part.shape[0]
     own_grad = (grad_sum1[:count] + own_part).astype(low)
     other_grad = (grad_sum1[count:] + other_part).astype(low)
@@ -840,16 +895,15 @@
         place,
     )
 
-    up_rows = reduced[shard : shard + wide].reshape(up_chunks, shard, width)
-    tail = reduced[shard + 2 * wide]
+    tail = rest_mine[shard]
     parts = [tail[at * shard : (at + 1) * shard] for at in range(6)]
     return (
         output,
         input_grad,
         grad_qkv,
-        reduced[:shard],
-        up_rows.transpose(1, 0, 2).reshape(shard, -1),
-        reduced[shard + wide : shard + 2 * wide],
+        rest_mine[:shard],
+        up_mine,
+        down_mine,
         grad_query_bias,
         grad_value_bias,
         parts[0],

time: 358 us -> 359 us (level)
  waiting for transfers between devices: 124 us -> 104 us
  other arithmetic: 28.1 us -> 42 us
  starting transfers between devices: 49.2 us -> 60.4 us
  matrix products: 36.1 us -> 29.8 us
    reduce_scatter x1 -> x0, waiting for transfers between devices: 13.2 us -> none  [local(): lax.psum_scatter(partial.reshape(-1, width), ('dp', 'seq'), scatter_dimen...]
    convert_element_type x2 -> x12, other arithmetic: 1.22 us -> 12.4 us  [add(): self.held = kept.astype(jnp.bfloat16) if self.left else kept]
    dot_general x7 -> x4, matrix products: 14.1 us -> 5.17 us  [weight_grad(): jnp.einsum('rk,rn->kn', left_rows, right_rows, preferred_element_type=jnp...]
    ppermute x32 -> x44, starting transfers between devices: 46 us -> 54.6 us  [swap(): return lax.ppermute(value, 'seq', [(i, i ^ bit) for i in range(16)])]
    reshape x7, local copies, waits for them, and re-layouts: 0.64 us -> 7.54 us  [local(): sums = jnp.concatenate([item.reshape(32, -1) for item in sums], axis=1)]
    concatenate x2 -> x0, local copies, waits for them, and re-layouts: 5.63 us -> none  [the longest x1 4.81 us: local(): small = jnp.concatenate(vectors + (up_bias,))]
    unnamed x60 -> x77, local copies, waits for them, and re-layouts: 9.6 us -> 4.19 us
    dynamic_slice x0 -> x4, local copies, waits for them, and re-layouts: none -> 5.18 us  [take(): return lax.dynamic_index_in_dim(value, index, axis, keepdims=False)]
  transfers between devices with their start and end apart: 36 -> 50, of which waited for: 26 -> 26; matrix products, arithmetic and copies ran while one was open for 15% -> 22% of each run, Pallas kernels for 16% -> 16%
where the time goes in v2:
time: 359 us; the launch traced here: 352 us
  waiting for transfers between devices  104 us (29%)
  starting transfers between devices  60.4 us (17%)
  Pallas kernels  55.8 us (16%)
  local copies, waits for them, and re-layouts  44.8 us (12%)
  other arithmetic  42 us (12%)
  matrix products  29.8 us (8%)
  between operations  15.5 us (4%)
    ppermute x44, waiting for transfers between devices, swap(): return lax.ppermute(value, 'seq', [(i, i ^ bit) for i in range(16)])  97.5 us
    ppermute x44, starting transfers between devices, swap(): return lax.ppermute(value, 'seq', [(i, i ^ bit) for i in range(16)])  54.6 us
    pallas_call x1, Pallas kernels, attend_group_back(): pl.pallas_call(attend_back_kernel, grid=(rows // QROWS,), in_specs=[pl.Bl...  31.5 us
    pallas_call x1, Pallas kernels, attend_group(): pl.pallas_call(attend_kernel, grid=(rows // QROWS,), in_specs=[pl.BlockSp...  24.3 us
    convert_element_type x12, other arithmetic, add(): self.held = kept.astype(jnp.bfloat16) if self.left else kept  12.4 us
    dot_general x4, matrix products, data_grad(): jnp.einsum('rn,kn->rk', grad_rows, weight_full, preferred_element_type=jn...  10.3 us
    dot_general x1, matrix products, local(): inner = jnp.dot(hidden_low, up_full, preferred_element_type=f32) + up_b  7.79 us
    reshape x7, local copies, waits for them, and re-layouts, local(): sums = jnp.concatenate([item.reshape(32, -1) for item in sums], axis=1)  7.54 us
  transfers between devices with their start and end apart: 50, of which 26 were waited for; matrix products, arithmetic and copies ran while one was open for 22% of the time, Pallas kernels for 16%

profile of v2, /device:TPU:0, one launch (start us, length us, event | category | flops | bytes accessed | tf_op | source)
XLA Modules:
  0.0 352.4 jit_solution(3451451519634813231)
XLA Ops:
  12.9 3.0 collective-permute-start.5
  15.9 2.4 collective-permute-done.5
  20.6 2.7 collective-permute-start
  23.8 3.3 collective-permute-start.7
  27.1 13.8 %collective-permute-done = bf16[128,768]{1,0:T(8,128)(2,1)S(1)} collective-permute-done((bf16[128,768]{1,0:T(8,128)(2,1)S(1)}, bf16[128,768]{1,0:T(8,128)(2,1)S(1)}, u32[]{:S(2)}, u32[]{:S(2)}) %collective-permute-start) | collective-permute-done | bytes 196640 | tf_op jit(solution)/shard_map/ppermute | solution.py:410
  47.2 2.8 collective-permute-start.11
  52.0 4.8 %collective-permute-done.8 = bf16[2,2,2,32,576]{4,3,2,1,0:T(8,128)(2,1)S(1)} collective-permute-done((bf16[2,2,2,32,576]{4,3,2,1,0:T(8,128)(2,1)S(1)}, bf16[2,2,2,32,576]{4,3,2,1,0:T(8,128)(2,1)S(1)}, u32[]{:S(2)}, u32[]{:S(2)}) %collective-permute-start.8) | collective-permute-done | bytes 294944 | tf_op jit(solution)/shard_map/ppermute | solution.py:414
  58.7 8.9 %collective-permute-done.4 = bf16[512,384]{1,0:T(8,128)(2,1)S(1)} collective-permute-done((bf16[512,384]{1,0:T(8,128)(2,1)S(1)}, bf16[512,384]{1,0:T(8,128)(2,1)S(1)}, u32[]{:S(2)}, u32[]{:S(2)}) %collective-permute-start.4) | collective-permute-done | bytes 393248 | tf_op jit(solution)/shard_map/ppermute | solution.py:410
  77.6 3.3 pad_maximum_fusion.4
  80.9 24.3 %shard_map.271 = (bf16[1024,192]{1,0:T(8,128)(2,1)}, f32[8,1024]{1,0:T(8,128)}) custom-call(bf16[1024,192]{1,0:T(8,128)(2,1)} %fusion.16.q_ref, bf16[2048,192]{1,0:T(8,128)(2,1)} %get-tuple-element.112.k_ref, bf16[2048,192]{1,0:T(8,128)(2,1)} %get-tuple-element.111.v_ref, s32[1024,1]{1,0:T(8,128)} %copy.60.qseg_ref, s32[1,2048]{1,0:T(1,128)} %pad_add_fusion.1.kseg_ref), custom_call_target="tpu_custom_call" | custom-call | flops 6442450944 | bytes 2359296 | tf_op jit(solution)/shard_map/pallas_call | solution.py:463
  106.2 2.4 collective-permute-start.15
  109.1 3.5 %collective-permute-done.15 = bf16[256,192]{1,0:T(8,128)(2,1)S(1)} collective-permute-done((bf16[256,192]{1,0:T(8,128)(2,1)S(1)}, bf16[256,192]{1,0:T(8,128)(2,1)S(1)}, u32[]{:S(2)}, u32[]{:S(2)}) %collective-permute-start.15) | collective-permute-done | bytes 98336 | tf_op jit(solution)/shard_map/ppermute | solution.py:410
  118.4 2.7 collective-permute-done.17
  125.4 4.8 %slice.349 = bf16[32,96,768]{2,1,0:T(8,128)(2,1)} slice(bf16[32,224,768]{2,1,0:T(8,128)(2,1)} %bitcast.268), slice={[0:32], [120:216], [0:768]} | slice | bytes 9437184 | tf_op jit(solution)/shard_map/slice | solution.py:806
  130.2 4.5 %fusion.93 = (bf16[32,24,768]{2,1,0:T(8,128)(2,1)S(1)}, bf16[32,24,768]{2,1,0:T(8,128)(2,1)S(1)}, bf16[32,24,768]{2,1,0:T(8,128)(2,1)}, bf16[32,24,768]{2,1,0:T(8,128)(2,1)}, bf16[32,24,768]{2,1,0:T(8,128)(2,1)}) fusion(bf16[32,224,768]{2,1,0:T(8,128)(2,1)} %bitcast.269), kind=kLoop, calls=%fused_computation.306 | loop fusion | bytes 11796480 | tf_op jit(solution)/shard_map/slice | solution.py:798
  138.4 7.8 %multiply_convert_fusion = (bf16[256,3072]{1,0:T(8,128)(2,1)S(1)}, f32[256,3072]{1,0:T(8,128)S(1)}, f32[256,3072]{1,0:T(8,128)S(1)}) fusion(f32[3072]{0:T(1024)S(1)} %copy-done.31, bf16[768,768]{1,0:T(8,128)(2,1)S(1)} %bitcast.292, bf16[768,768]{1,0:T(8,128)(2,1)S(1)} %bitcast.294, bf16[768,768]{1,0:T(8,128)(2,1)S(1)} %bitcast.296, ...), kind=kOutput, calls=%fused_computation.13 | convolution fusion | flops 1279721472 | bytes 13389824 | tf_op jit(solution)/shard_map/dot_general | solution.py:818
  151.9 3.1 multiply_reduce_fusion
  180.1 8.7 %collective-permute-done.19 = bf16[128,768]{1,0:T(8,128)(2,1)S(1)} collective-permute-done((bf16[128,768]{1,0:T(8,128)(2,1)S(1)}, bf16[128,768]{1,0:T(8,128)(2,1)S(1)}, u32[]{:S(2)}, u32[]{:S(2)}) %collective-permute-start.19) | collective-permute-done | bytes 196640 | tf_op jit(solution)/shard_map/ppermute | solution.py:410
  190.7 3.4 collective-permute-done.20
  195.8 4.1 %collective-permute-done.22 = bf16[256,192]{1,0:T(8,128)(2,1)S(1)} collective-permute-done((bf16[256,192]{1,0:T(8,128)(2,1)S(1)}, bf16[256,192]{1,0:T(8,128)(2,1)S(1)}, u32[]{:S(2)}, u32[]{:S(2)}) %collective-permute-start.22) | collective-permute-done | bytes 98336 | tf_op jit(solution)/shard_map/ppermute | solution.py:410
  203.7 3.7 %fusion = bf16[2,2,2,2,24,3072]{5,4,1,2,3,0:T(8,128)(2,1)S(1)} fusion(bf16[2,2,2,2,24,3072]{5,4,1,2,3,0:T(8,128)(2,1)} %collective-permute-done.24, bf16[2,2,2,2,1,24,3072]{6,5,4,3,2,1,0:T(8,128)(2,1)S(1)} %get-tuple-element.101), kind=kLoop, calls=%fused_computation.5 | loop fusion | flops 4718592 | bytes 7077888 | tf_op jit(solution)/shard_map/convert_element_type | solution.py:704
  211.6 31.5 %shard_map.272 = (bf16[1024,192]{1,0:T(8,128)(2,1)}, f32[2048,192]{1,0:T(8,128)}, f32[2048,192]{1,0:T(8,128)}) custom-call(bf16[1024,192]{1,0:T(8,128)(2,1)} %fusion.16.q_ref, bf16[2048,192]{1,0:T(8,128)(2,1)} %get-tuple-element.112.k_ref, bf16[2048,192]{1,0:T(8,128)(2,1)} %get-tuple-element.111.v_ref, bf16[1024,192]{1,0:T(8,128)(2,1)} %pad_maximum_fusion.10.grad_ref, ...), custom_call_target="tpu_custom_call" | custom-call | flops 16106127360 | bytes 4718592 | tf_op jit(solution)/shard_map/pallas_call | solution.py:534
  257.7 3.2 fusion.103
  269.8 6.1 %collective-permute-done.31 = bf16[512,384]{1,0:T(8,128)(2,1)} collective-permute-done((bf16[512,384]{1,0:T(8,128)(2,1)}, bf16[512,384]{1,0:T(8,128)(2,1)}, u32[]{:S(2)}, u32[]{:S(2)}) %collective-permute-start.31) | collective-permute-done | bytes 393248 | tf_op jit(solution)/shard_map/ppermute | solution.py:410
  291.1 9.8 %collective-permute-done.36 = bf16[256,384]{1,0:T(8,128)(2,1)S(1)} collective-permute-done((bf16[256,384]{1,0:T(8,128)(2,1)S(1)}, bf16[256,384]{1,0:T(8,128)(2,1)S(1)}, u32[]{:S(2)}, u32[]{:S(2)}) %collective-permute-start.36) | collective-permute-done | bytes 196640 | tf_op jit(solution)/shard_map/ppermute | solution.py:410
  301.1 2.4 collective-permute-start.43
  309.8 11.0 %collective-permute-done.43 = bf16[32,768]{1,0:T(8,128)(2,1)S(1)} collective-permute-done((bf16[32,768]{1,0:T(8,128)(2,1)S(1)}, bf16[32,768]{1,0:T(8,128)(2,1)S(1)}, u32[]{:S(2)}, u32[]{:S(2)}) %collective-permute-start.43) | collective-permute-done | bytes 49184 | tf_op jit(solution)/shard_map/ppermute | solution.py:410
  320.8 3.2 collective-permute-done.42
  324.0 3.2 collective-permute-done.41
  327.1 4.2 %collective-permute-done.40 = bf16[128,768]{1,0:T(8,128)(2,1)S(1)} collective-permute-done((bf16[128,768]{1,0:T(8,128)(2,1)S(1)}, bf16[128,768]{1,0:T(8,128)(2,1)S(1)}, u32[]{:S(2)}, u32[]{:S(2)}) %collective-permute-start.40) | collective-permute-done | bytes 196640 | tf_op jit(solution)/shard_map/ppermute | solution.py:410
  335.6 3.2 collective-permute-done.47
  340.8 2.6 collective-permute-done.48
  (335 shorter events, 138.5 us)
Async XLA Ops:
  7.2 117.2 %all-gather.3.cloned.1.call-start = ((), (), s32[]{:S(2)}) async-start(), calls=%async_computation | async-start | bytes 11354112 | tf_op jit(solution)/shard_map/all_gather | solution.py:777
  20.6 20.2 %collective-permute-start = (bf16[128,768]{1,0:T(8,128)(2,1)S(1)}, bf16[128,768]{1,0:T(8,128)(2,1)S(1)}, u32[]{:S(2)}, u32[]{:S(2)}) collective-permute-start(bf16[128,768]{1,0:T(8,128)(2,1)S(1)} %get-tuple-element.138), channel_id=1, source_target_pairs={{0,8},{1,9},{2,10},{3,11},{4,12},{5,13},{6,14},{7,15},{8,0},{9,1},... | collective-permute-start | bytes 589832 | tf_op jit(solution)/shard_map/ppermute | solution.py:410
  23.8 21.7 %collective-permute-start.7 = (bf16[2,2,32,576]{3,2,1,0:T(8,128)(2,1)S(1)}, bf16[2,2,32,576]{3,2,1,0:T(8,128)(2,1)S(1)}, u32[]{:S(2)}, u32[]{:S(2)}) collective-permute-start(bf16[2,2,32,576]{3,2,1,0:T(8,128)(2,1)S(1)} %pad_maximum_fusion.29), channel_id=1, source_target_pairs={{0,8},{1,9},{2,10},{3,11},{4,12},{5,13},{6,14},{7,15},{8,0},{9,1},... | collective-permute-start | bytes 442376 | tf_op jit(solution)/shard_map/ppermute | solution.py:410
  45.6 11.2 %collective-permute-start.8 = (bf16[2,2,2,32,576]{4,3,2,1,0:T(8,128)(2,1)S(1)}, bf16[2,2,2,32,576]{4,3,2,1,0:T(8,128)(2,1)S(1)}, u32[]{:S(2)}, u32[]{:S(2)}) collective-permute-start(bf16[2,2,2,32,576]{4,3,2,1,0:T(8,128)(2,1)S(1)} %pad_maximum_fusion.21), channel_id=1, source_target_pairs={{0,16},{16,0},{1,17},{17,1},{2,18},{18,2},{3,19},{19,3},{4,20},{20... | collective-permute-start | bytes 884744 | tf_op jit(solution)/shard_map/ppermute | solution.py:414
  47.2 9.9 %collective-permute-start.11 = (s32[128]{0:T(128)S(1)}, s32[128]{0:T(128)S(1)}, u32[]{:S(2)}, u32[]{:S(2)}) collective-permute-start(s32[128]{0:T(128)S(1)} %get-tuple-element.169), channel_id=1, source_target_pairs={{0,8},{1,9},{2,10},{3,11},{4,12},{5,13},{6,14},{7,15},{8,0},{9,1},... | collective-permute-start | bytes 1544 | tf_op jit(solution)/shard_map/ppermute | solution.py:410
  50.0 17.6 %collective-permute-start.2 = (bf16[512,384]{1,0:T(8,128)(2,1)S(1)}, bf16[512,384]{1,0:T(8,128)(2,1)S(1)}, u32[]{:S(2)}, u32[]{:S(2)}) collective-permute-start(bf16[512,384]{1,0:T(8,128)(2,1)S(1)} %pad_maximum_fusion.13), channel_id=1, source_target_pairs={{0,4},{1,5},{2,6},{3,7},{4,0},{5,1},{6,2},{7,3},{8,12},{9,13},{10,... | collective-permute-start | bytes 1179656 | tf_op jit(solution)/shard_map/ppermute | solution.py:410
  50.4 17.2 %collective-permute-start.4 = (bf16[512,384]{1,0:T(8,128)(2,1)S(1)}, bf16[512,384]{1,0:T(8,128)(2,1)S(1)}, u32[]{:S(2)}, u32[]{:S(2)}) collective-permute-start(bf16[512,384]{1,0:T(8,128)(2,1)S(1)} %pad_maximum_fusion.14), channel_id=1, source_target_pairs={{0,2},{1,3},{2,0},{3,1},{4,6},{5,7},{6,4},{7,5},{8,10},{9,11},{10,... | collective-permute-start | bytes 1179656 | tf_op jit(solution)/shard_map/ppermute | solution.py:410
  57.0 10.8 %collective-permute-start.9 = (bf16[2,2,2,2,32,576]{5,4,3,2,1,0:T(8,128)(2,1)S(1)}, bf16[2,2,2,2,32,576]{5,4,3,2,1,0:T(8,128)(2,1)S(1)}, u32[]{:S(2)}, u32[]{:S(2)}) collective-permute-start(bf16[2,2,2,2,32,576]{5,4,3,2,1,0:T(8,128)(2,1)S(1)} %pad_maximum_fusion.9), channel_id=1, source_target_pairs={{0,1},{1,0},{2,3},{3,2},{4,5},{5,4},{6,7},{7,6},{8,9},{9,8},{10,11... | collective-permute-start | bytes 1769480 | tf_op jit(solution)/shard_map/ppermute | solution.py:410
  57.1 13.6 %collective-permute-start.12 = (s32[1,256]{1,0:T(1,128)S(1)}, s32[1,256]{1,0:T(1,128)S(1)}, u32[]{:S(2)}, u32[]{:S(2)}) collective-permute-start(s32[1,256]{1,0:T(1,128)S(1)} %bitcast.309), channel_id=1, source_target_pairs={{0,2},{1,3},{2,0},{3,1},{4,6},{5,7},{6,4},{7,5},{8,10},{9,11},{10,... | collective-permute-start | bytes 3080 | tf_op jit(solution)/shard_map/ppermute | solution.py:410
  123.7 12.6 %collective-permute-start.18 = (bf16[128,768]{1,0:T(8,128)(2,1)}, bf16[128,768]{1,0:T(8,128)(2,1)S(1)}, u32[]{:S(2)}, u32[]{:S(2)}) collective-permute-start(bf16[128,768]{1,0:T(8,128)(2,1)} %get-tuple-element.133), channel_id=1, source_target_pairs={{0,8},{1,9},{2,10},{3,11},{4,12},{5,13},{6,14},{7,15},{8,0},{9,1},... | collective-permute-start | bytes 589832 | tf_op jit(solution)/shard_map/ppermute | solution.py:410
  163.8 37.0 %collective-permute-start.23 = (bf16[2,2,2,2,96,768]{5,4,1,2,0,3:T(8,128)(2,1)}, bf16[2,2,2,2,96,768]{5,4,1,2,0,3:T(8,128)(2,1)}, u32[]{:S(2)}, u32[]{:S(2)}) collective-permute-start(bf16[2,2,2,2,96,768]{5,4,1,2,0,3:T(8,128)(2,1)} %bitcast.261), channel_id=1, source_target_pairs={{0,1},{1,0},{2,3},{3,2},{4,5},{5,4},{6,7},{7,6},{8,9},{9,8},{10,11... | collective-permute-start | bytes 7077896 | tf_op jit(solution)/shard_map/ppermute | solution.py:410
  163.8 37.0 %collective-permute-start.24 = (bf16[2,2,2,2,24,3072]{5,4,1,2,3,0:T(8,128)(2,1)}, bf16[2,2,2,2,24,3072]{5,4,1,2,3,0:T(8,128)(2,1)}, u32[]{:S(2)}, u32[]{:S(2)}) collective-permute-start(bf16[2,2,2,2,24,3072]{5,4,1,2,3,0:T(8,128)(2,1)} %bitcast.260), channel_id=1, source_target_pairs={{0,1},{1,0},{2,3},{3,2},{4,5},{5,4},{6,7},{7,6},{8,9},{9,8},{10,11... | collective-permute-start | bytes 7077896 | tf_op jit(solution)/shard_map/ppermute | solution.py:410
  176.8 12.0 %collective-permute-start.19 = (bf16[128,768]{1,0:T(8,128)(2,1)S(1)}, bf16[128,768]{1,0:T(8,128)(2,1)S(1)}, u32[]{:S(2)}, u32[]{:S(2)}) collective-permute-start(bf16[128,768]{1,0:T(8,128)(2,1)S(1)} %get-tuple-element.129), channel_id=1, source_target_pairs={{0,8},{1,9},{2,10},{3,11},{4,12},{5,13},{6,14},{7,15},{8,0},{9,1},... | collective-permute-start | bytes 589832 | tf_op jit(solution)/shard_map/ppermute | solution.py:410
  180.0 20.8 %collective-permute-start.25 = (bf16[2,2,2,2,32,768]{5,4,1,0,3,2:T(8,128)(2,1)S(1)}, bf16[2,2,2,2,32,768]{5,4,1,0,3,2:T(8,128)(2,1)S(1)}, u32[]{:S(2)}, u32[]{:S(2)}) collective-permute-start(bf16[2,2,2,2,32,768]{5,4,1,0,3,2:T(8,128)(2,1)S(1)} %bitcast.302), channel_id=1, source_target_pairs={{0,1},{1,0},{2,3},{3,2},{4,5},{5,4},{6,7},{7,6},{8,9},{9,8},{10,11... | collective-permute-start | bytes 2359304 | tf_op jit(solution)/shard_map/ppermute | solution.py:410
  201.1 42.0 %collective-permute-start.28 = (bf16[2,2,2,32,768]{4,3,1,0,2:T(8,128)(2,1)S(1)}, bf16[2,2,2,32,768]{4,3,1,0,2:T(8,128)(2,1)S(1)}, u32[]{:S(2)}, u32[]{:S(2)}) collective-permute-start(bf16[2,2,2,32,768]{4,3,1,0,2:T(8,128)(2,1)S(1)} %dynamic-slice_bitcast_fusion.4), channel_id=1, source_target_pairs={{0,4},{1,5},{2,6},{3,7},{4,0},{5,1},{6,2},{7,3},{8,12},{9,13},{10,... | collective-permute-start | bytes 1179656 | tf_op jit(solution)/shard_map/ppermute | solution.py:410
  208.8 34.3 %collective-permute-start.27 = (bf16[2,2,2,24,3072]{4,3,0,1,2:T(8,128)(2,1)S(1)}, bf16[2,2,2,24,3072]{4,3,0,1,2:T(8,128)(2,1)}, u32[]{:S(2)}, u32[]{:S(2)}) collective-permute-start(bf16[2,2,2,24,3072]{4,3,0,1,2:T(8,128)(2,1)S(1)} %dynamic-slice_bitcast_fusion), channel_id=1, source_target_pairs={{0,16},{16,0},{1,17},{17,1},{2,18},{18,2},{3,19},{19,3},{4,20},{20... | collective-permute-start | bytes 3538952 | tf_op jit(solution)/shard_map/ppermute | solution.py:414
  210.2 32.9 %collective-permute-start.26 = (bf16[2,2,2,96,768]{4,3,1,2,0:T(8,128)(2,1)S(1)}, bf16[2,2,2,96,768]{4,3,1,2,0:T(8,128)(2,1)S(1)}, u32[]{:S(2)}, u32[]{:S(2)}) collective-permute-start(bf16[2,2,2,96,768]{4,3,1,2,0:T(8,128)(2,1)S(1)} %dynamic-slice_bitcast_fusion.1), channel_id=1, source_target_pairs={{0,2},{1,3},{2,0},{3,1},{4,6},{5,7},{6,4},{7,5},{8,10},{9,11},{10,... | collective-permute-start | bytes 3538952 | tf_op jit(solution)/shard_map/ppermute | solution.py:410
  245.5 22.1 %collective-permute-start.34 = (bf16[2,2,32,768]{3,2,1,0:T(8,128)(2,1)S(1)}, bf16[2,2,32,768]{3,2,1,0:T(8,128)(2,1)}, u32[]{:S(2)}, u32[]{:S(2)}) collective-permute-start(bf16[2,2,32,768]{3,2,1,0:T(8,128)(2,1)S(1)} %dynamic-slice_bitcast_fusion.8), channel_id=1, source_target_pairs={{0,2},{1,3},{2,0},{3,1},{4,6},{5,7},{6,4},{7,5},{8,10},{9,11},{10,... | collective-permute-start | bytes 589832 | tf_op jit(solution)/shard_map/ppermute | solution.py:410
  251.6 16.5 %collective-permute-start.33 = (bf16[2,2,24,3072]{3,2,0,1:T(8,128)(2,1)}, bf16[2,2,24,3072]{3,2,0,1:T(8,128)(2,1)}, u32[]{:S(2)}, u32[]{:S(2)}) collective-permute-start(bf16[2,2,24,3072]{3,2,0,1:T(8,128)(2,1)} %dynamic-slice_bitcast_fusion.2), channel_id=1, source_target_pairs={{0,2},{1,3},{2,0},{3,1},{4,6},{5,7},{6,4},{7,5},{8,10},{9,11},{10,... | collective-permute-start | bytes 1769480 | tf_op jit(solution)/shard_map/ppermute | solution.py:410
  254.2 15.6 %collective-permute-start.32 = (bf16[2,2,96,768]{3,2,0,1:T(8,128)(2,1)}, bf16[2,2,96,768]{3,2,0,1:T(8,128)(2,1)}, u32[]{:S(2)}, u32[]{:S(2)}) collective-permute-start(bf16[2,2,96,768]{3,2,0,1:T(8,128)(2,1)} %dynamic-slice_bitcast_fusion.3), channel_id=1, source_target_pairs={{0,16},{16,0},{1,17},{17,1},{2,18},{18,2},{3,19},{19,3},{4,20},{20... | collective-permute-start | bytes 1769480 | tf_op jit(solution)/shard_map/ppermute | solution.py:414
  262.6 13.3 %collective-permute-start.31 = (bf16[512,384]{1,0:T(8,128)(2,1)}, bf16[512,384]{1,0:T(8,128)(2,1)}, u32[]{:S(2)}, u32[]{:S(2)}) collective-permute-start(bf16[512,384]{1,0:T(8,128)(2,1)} %pad_maximum_fusion.18), channel_id=1, source_target_pairs={{0,2},{1,3},{2,0},{3,1},{4,6},{5,7},{6,4},{7,5},{8,10},{9,11},{10,... | collective-permute-start | bytes 1179656 | tf_op jit(solution)/shard_map/ppermute | solution.py:410
  263.3 12.6 %collective-permute-start.30 = (bf16[512,384]{1,0:T(8,128)(2,1)}, bf16[512,384]{1,0:T(8,128)(2,1)}, u32[]{:S(2)}, u32[]{:S(2)}) collective-permute-start(bf16[512,384]{1,0:T(8,128)(2,1)} %slice.367), channel_id=1, source_target_pairs={{0,4},{1,5},{2,6},{3,7},{4,0},{5,1},{6,2},{7,3},{8,12},{9,13},{10,... | collective-permute-start | bytes 1179656 | tf_op jit(solution)/shard_map/ppermute | solution.py:410
  267.6 19.2 %collective-permute-start.44 = (bf16[16,32,576]{2,1,0:T(8,128)(2,1)S(1)}, bf16[16,32,576]{2,1,0:T(8,128)(2,1)S(1)}, u32[]{:S(2)}, u32[]{:S(2)}) collective-permute-start(bf16[16,32,576]{2,1,0:T(8,128)(2,1)S(1)} %fusion.35), channel_id=1, source_target_pairs={{0,1},{1,0},{2,3},{3,2},{4,5},{5,4},{6,7},{7,6},{8,9},{9,8},{10,11... | collective-permute-start | bytes 1769480 | tf_op jit(solution)/shard_map/ppermute | solution.py:410
  281.9 19.0 %collective-permute-start.38 = (bf16[2,24,3072]{2,1,0:T(8,128)(2,1)S(1)}, bf16[2,24,3072]{2,1,0:T(8,128)(2,1)S(1)}, u32[]{:S(2)}, u32[]{:S(2)}) collective-permute-start(bf16[2,24,3072]{2,1,0:T(8,128)(2,1)S(1)} %dynamic-slice_bitcast_fusion.6), channel_id=1, source_target_pairs={{0,4},{1,5},{2,6},{3,7},{4,0},{5,1},{6,2},{7,3},{8,12},{9,13},{10,... | collective-permute-start | bytes 884744 | tf_op jit(solution)/shard_map/ppermute | solution.py:410
  285.3 15.7 %collective-permute-start.37 = (bf16[2,96,768]{2,1,0:T(8,128)(2,1)S(1)}, bf16[2,96,768]{2,1,0:T(8,128)(2,1)S(1)}, u32[]{:S(2)}, u32[]{:S(2)}) collective-permute-start(bf16[2,96,768]{2,1,0:T(8,128)(2,1)S(1)} %dynamic-slice_bitcast_fusion.7), channel_id=1, source_target_pairs={{0,4},{1,5},{2,6},{3,7},{4,0},{5,1},{6,2},{7,3},{8,12},{9,13},{10,... | collective-permute-start | bytes 884744 | tf_op jit(solution)/shard_map/ppermute | solution.py:410
  286.8 14.1 %collective-permute-start.36 = (bf16[256,384]{1,0:T(8,128)(2,1)S(1)}, bf16[256,384]{1,0:T(8,128)(2,1)S(1)}, u32[]{:S(2)}, u32[]{:S(2)}) collective-permute-start(bf16[256,384]{1,0:T(8,128)(2,1)S(1)} %slice.482), channel_id=1, source_target_pairs={{0,4},{1,5},{2,6},{3,7},{4,0},{5,1},{6,2},{7,3},{8,12},{9,13},{10,... | collective-permute-start | bytes 589832 | tf_op jit(solution)/shard_map/ppermute | solution.py:410
  289.0 18.4 %collective-permute-start.45 = (bf16[8,32,576]{2,1,0:T(8,128)(2,1)S(1)}, bf16[8,32,576]{2,1,0:T(8,128)(2,1)S(1)}, u32[]{:S(2)}, u32[]{:S(2)}) collective-permute-start(bf16[8,32,576]{2,1,0:T(8,128)(2,1)S(1)} %dynamic-slice_bitcast_fusion.5), channel_id=1, source_target_pairs={{0,16},{16,0},{1,17},{17,1},{2,18},{18,2},{3,19},{19,3},{4,20},{20... | collective-permute-start | bytes 884744 | tf_op jit(solution)/shard_map/ppermute | solution.py:414
  301.1 19.7 %collective-permute-start.43 = (bf16[32,768]{1,0:T(8,128)(2,1)S(1)}, bf16[32,768]{1,0:T(8,128)(2,1)S(1)}, u32[]{:S(2)}, u32[]{:S(2)}) collective-permute-start(bf16[32,768]{1,0:T(8,128)(2,1)S(1)} %dynamic-slice_bitcast_fusion.18), channel_id=1, source_target_pairs={{0,8},{1,9},{2,10},{3,11},{4,12},{5,13},{6,14},{7,15},{8,0},{9,1},... | collective-permute-start | bytes 147464 | tf_op jit(solution)/shard_map/ppermute | solution.py:410
  303.5 20.4 %collective-permute-start.42 = (bf16[24,3072]{1,0:T(8,128)(2,1)S(1)}, bf16[24,3072]{1,0:T(8,128)(2,1)S(1)}, u32[]{:S(2)}, u32[]{:S(2)}) collective-permute-start(bf16[24,3072]{1,0:T(8,128)(2,1)S(1)} %dynamic-slice_bitcast_fusion.14), channel_id=1, source_target_pairs={{0,8},{1,9},{2,10},{3,11},{4,12},{5,13},{6,14},{7,15},{8,0},{9,1},... | collective-permute-start | bytes 442376 | tf_op jit(solution)/shard_map/ppermute | solution.py:410
  304.2 22.9 %collective-permute-start.41 = (bf16[96,768]{1,0:T(8,128)(2,1)S(1)}, bf16[96,768]{1,0:T(8,128)(2,1)S(1)}, u32[]{:S(2)}, u32[]{:S(2)}) collective-permute-start(bf16[96,768]{1,0:T(8,128)(2,1)S(1)} %dynamic-slice_bitcast_fusion.15), channel_id=1, source_target_pairs={{0,8},{1,9},{2,10},{3,11},{4,12},{5,13},{6,14},{7,15},{8,0},{9,1},... | collective-permute-start | bytes 442376 | tf_op jit(solution)/shard_map/ppermute | solution.py:410
  306.7 24.7 %collective-permute-start.40 = (bf16[128,768]{1,0:T(8,128)(2,1)S(1)}, bf16[128,768]{1,0:T(8,128)(2,1)S(1)}, u32[]{:S(2)}, u32[]{:S(2)}) collective-permute-start(bf16[128,768]{1,0:T(8,128)(2,1)S(1)} %fusion.45), channel_id=1, source_target_pairs={{0,8},{1,9},{2,10},{3,11},{4,12},{5,13},{6,14},{7,15},{8,0},{9,1},... | collective-permute-start | bytes 589832 | tf_op jit(solution)/shard_map/ppermute | solution.py:410
  307.5 26.8 %collective-permute-start.46 = (bf16[4,32,576]{2,1,0:T(8,128)(2,1)S(1)}, bf16[4,32,576]{2,1,0:T(8,128)(2,1)S(1)}, u32[]{:S(2)}, u32[]{:S(2)}) collective-permute-start(bf16[4,32,576]{2,1,0:T(8,128)(2,1)S(1)} %dynamic-slice_bitcast_fusion.13), channel_id=1, source_target_pairs={{0,8},{1,9},{2,10},{3,11},{4,12},{5,13},{6,14},{7,15},{8,0},{9,1},... | collective-permute-start | bytes 442376 | tf_op jit(solution)/shard_map/ppermute | solution.py:410
  (57 other events, 381.7 us)
Sparse Core Ops, SparseCore 0:
  11.5 106.6 all-gather.2
